TPU v7x, 512 devices: a whole 4x4x16 slice. The times are simulated.
512 devices in a mesh: ctx: 64 (over y_hi, z, core), head: 8 (over x, y_lo).
Axes of the slice: x: 4, y: 4 (y_hi: 2, y_lo: 2; y = y_hi * 2 + y_lo), z: 16, core: 2. Of those that a mesh axis runs over, the one named last changes fastest.
Arguments:
- query_rows: bfloat16 [16384, 1024], P(('ctx', 'head')), may hold values from -30 to 30
- key_rows: bfloat16 [16384, 1024], P(('ctx', 'head')), may hold values from -7.2 to 7.2
- value_rows: bfloat16 [16384, 1024], P(('ctx', 'head')), may hold values from -6 to 6
- cotangent: bfloat16 [16384, 1024], P(('ctx', 'head')), may hold values from -3 to 3
- key_taps: float32 [3, 1024], P(None, 'head'), may hold values from 0.2 to 1
- value_taps: float32 [3, 1024], P(None, 'head'), may hold values from 0.2 to 1
Outputs:
- attended: bfloat16 [16384, 1024], P(('ctx', 'head'))
- grad_query: bfloat16 [16384, 1024], P(('ctx', 'head'))
- grad_key: bfloat16 [16384, 1024], P(('ctx', 'head'))
- grad_value: bfloat16 [16384, 1024], P(('ctx', 'head'))
- grad_key_taps: float32 [3, 1024], P(None, 'head')
- grad_value_taps: float32 [3, 1024], P(None, 'head')
All inputs are finite; a program needn't handle non-finite values.
Results may differ from a plain program's by a relative error of at most 0.012.
Values may be sent and summed in bfloat16 or wider, within the bound.
A program may use at most 128 MiB of HBM per device.

v0:
```python
import jax
import jax.numpy as jnp
from jax import lax
from jax.sharding import PartitionSpec as P

D = 1024
HEADS = 16


def from_behind(array, axis, by):
    devices = lax.axis_size(axis)
    pairs = [(i, i + by) for i in range(devices) if 0 <= i + by < devices]
    return lax.ppermute(array, axis, pairs)


def compress(row_data, tap_weights, rim_row):
    channels = row_data.shape[1]
    grouped = row_data.astype(jnp.float32).reshape(-1, 4, channels)
    before = jnp.concatenate([rim_row.astype(jnp.float32)[None, :], grouped[:-1, 3]], axis=0)
    packed = (
        tap_weights[0] * before + tap_weights[1] * grouped[:, 0] + tap_weights[2] * grouped[:, 1]
    ).astype(jnp.bfloat16)
    return (packed, grouped, before)


def spread_back(comp_grads, tap_weights, incoming, grouped, before):
    channels = comp_grads.shape[1]
    tail_rows = jnp.concatenate(
        [tap_weights[0] * comp_grads[1:], incoming.astype(jnp.float32)[None, :]], axis=0
    )
    spread = jnp.stack(
        [
            tap_weights[1] * comp_grads,
            tap_weights[2] * comp_grads,
            jnp.zeros_like(comp_grads),
            tail_rows,
        ],
        axis=1,
    )
    tap_terms = jnp.stack(
        [
            jnp.sum(comp_grads * before, axis=0),
            jnp.sum(comp_grads * grouped[:, 0], axis=0),
            jnp.sum(comp_grads * grouped[:, 1], axis=0),
        ]
    )
    return (spread.reshape(-1, channels).astype(jnp.bfloat16), tap_terms)


def local(query_rows, key_rows, value_rows, cotangent, key_taps, value_taps):
    query_loc, key_loc, value_loc, cot_loc = (
        lax.all_to_all(query_rows, "head", split_axis=1, concat_axis=0, tiled=True),
        lax.all_to_all(key_rows, "head", split_axis=1, concat_axis=0, tiled=True),
        lax.all_to_all(value_rows, "head", split_axis=1, concat_axis=0, tiled=True),
        lax.all_to_all(cotangent, "head", split_axis=1, concat_axis=0, tiled=True),
    )
    length, channels = query_loc.shape
    head_dim = D // HEADS
    local_heads = channels // head_dim
    scaling = head_dim ** (-0.5)
    rim_rows = from_behind(jnp.stack([key_loc[-1], value_loc[-1]]), "ctx", 1)
    key_comp, key_groups, key_before = compress(key_loc, key_taps, rim_rows[0])
    value_comp, value_groups, value_before = compress(value_loc, value_taps, rim_rows[1])
    key_all, value_all = (
        lax.all_gather(key_comp, "ctx", axis=0, tiled=True),
        lax.all_gather(value_comp, "ctx", axis=0, tiled=True),
    )
    query_heads = query_loc.reshape(length, local_heads, head_dim)
    cot_heads = cot_loc.reshape(length, local_heads, head_dim)
    key_heads = key_all.reshape(-1, local_heads, head_dim)
    value_heads = value_all.reshape(-1, local_heads, head_dim)
    scores = (
        jnp.einsum("qhd,khd->hqk", query_heads, key_heads, preferred_element_type=jnp.float32)
        * scaling
    )
    row_max = jnp.max(scores, axis=2, keepdims=True)
    raised = jnp.exp(scores - row_max)
    row_total = jnp.sum(raised, axis=2, keepdims=True)
    weights = (raised / row_total).astype(jnp.bfloat16)
    attended_heads = jnp.einsum(
        "hqk,khd->qhd", weights, value_heads, preferred_element_type=jnp.float32
    ).astype(jnp.bfloat16)
    attended_loc = attended_heads.reshape(length, channels)
    attended = lax.all_to_all(attended_loc, "head", split_axis=0, concat_axis=1, tiled=True)
    offset = jnp.sum(cot_heads.astype(jnp.float32) * attended_heads.astype(jnp.float32), axis=2)
    dweights = jnp.einsum(
        "qhd,khd->hqk", cot_heads, value_heads, preferred_element_type=jnp.float32
    )
    dscores = (weights.astype(jnp.float32) * (dweights - offset.T[:, :, None])).astype(jnp.bfloat16)
    grad_query_loc = (
        (
            jnp.einsum("hqk,khd->qhd", dscores, key_heads, preferred_element_type=jnp.float32)
            * scaling
        )
        .astype(jnp.bfloat16)
        .reshape(length, channels)
    )
    number = length // 4 * lax.axis_size("ctx")
    key_part = (
        jnp.einsum("hqk,qhd->khd", dscores, query_heads, preferred_element_type=jnp.float32)
        * scaling
    )
    value_part = jnp.einsum("hqk,qhd->khd", weights, cot_heads, preferred_element_type=jnp.float32)
    summed = lax.psum_scatter(
        jnp.concatenate(
            [key_part.reshape(number, channels), value_part.reshape(number, channels)], axis=1
        ),
        "ctx",
        scatter_dimension=0,
        tiled=True,
    )
    grad_key_comp = summed[:, :channels]
    grad_value_comp = summed[:, channels:]
    outgoing = jnp.stack(
        [key_taps[0] * grad_key_comp[0], value_taps[0] * grad_value_comp[0]]
    ).astype(jnp.bfloat16)
    incoming = from_behind(outgoing, "ctx", -1)
    grad_key_loc, key_tap_terms = spread_back(
        grad_key_comp, key_taps, incoming[0], key_groups, key_before
    )
    grad_value_loc, value_tap_terms = spread_back(
        grad_value_comp, value_taps, incoming[1], value_groups, value_before
    )
    grad_key_taps, grad_value_taps = lax.psum((key_tap_terms, value_tap_terms), "ctx")
    grad_query, grad_key, grad_value = (
        lax.all_to_all(grad_query_loc, "head", split_axis=0, concat_axis=1, tiled=True),
        lax.all_to_all(grad_key_loc, "head", split_axis=0, concat_axis=1, tiled=True),
        lax.all_to_all(grad_value_loc, "head", split_axis=0, concat_axis=1, tiled=True),
    )
    return (attended, grad_query, grad_key, grad_value, grad_key_taps, grad_value_taps)


def solution(mesh):
    return jax.shard_map(
        local,
        mesh=mesh,
        in_specs=(
            P(("ctx", "head"), None),
            P(("ctx", "head"), None),
            P(("ctx", "head"), None),
            P(("ctx", "head"), None),
            P(None, "head"),
            P(None, "head"),
        ),
        out_specs=(
            P(("ctx", "head"), None),
            P(("ctx", "head"), None),
            P(("ctx", "head"), None),
            P(("ctx", "head"), None),
            P(None, "head"),
            P(None, "head"),
        ),
        check_vma=False,
    )
```

profile of v0, /device:TPU:1, one launch (start us, length us, event | category | flops | bytes accessed | tf_op | source)
XLA Modules:
  0.0 718.0 jit_solution(16662987119266013339)
XLA Ops:
  8.7 5.9 all-to-all-start
  16.0 3.6 all-to-all-done
  19.6 3.4 all-to-all-start.1
  23.8 4.2 all-to-all-done.1
  28.0 6.7 collective-permute-start
  38.7 3.4 all-to-all-start.2
  43.5 3.6 all-to-all-done.2
  47.1 3.4 all-to-all-start.4
  51.5 3.9 all-to-all-done.4
  56.4 125.1 %all-gather.5.cloned.1.call-done = bf16[4096,128]{1,0:T(8,128)(2,1)} async-done(((bf16[64,128]{1,0:T(8,128)(2,1)}), bf16[4096,128]{1,0:T(8,128)(2,1)}) %all-gather.5.cloned.1.call-update) | async-done | bytes 1048592 | tf_op jit(solution)/shard_map/all_gather | solution.py:65
  183.0 5.4 fusion.25
  188.5 4.1 divide_convert_fusion
  192.5 1.9 copy-done.1
  194.5 2.7 fusion.26
  197.2 124.9 %all-gather.3.cloned.1.call-done = bf16[4096,128]{1,0:T(8,128)(2,1)} async-done(((bf16[64,128]{1,0:T(8,128)(2,1)}), bf16[4096,128]{1,0:T(8,128)(2,1)}) %all-gather.3.cloned.1.call-update) | async-done | bytes 1048592 | tf_op jit(solution)/shard_map/all_gather | solution.py:66
  323.6 3.1 multiply_reduce_fusion
  328.5 1.9 copy-done.3
  330.5 2.7 convolution_multiply_fusion
  333.2 3.0 copy.136
  336.2 1.8 copy.137
  338.0 4.5 pad_maximum_fusion
  342.6 3.0 fusion.9
  346.4 4.0 all-to-all-start.5
  351.4 4.2 all-to-all-done.5
  355.6 3.4 all-to-all-start.3
  359.6 4.4 all-to-all-done.3
  364.6 185.6 %reduce-scatter.2.cloned.1.call-done = f32[64,256]{1,0:T(8,128)} async-done(((f32[4096,256]{1,0:T(8,128)}), f32[64,256]{1,0:T(8,128)}) %reduce-scatter.2.cloned.1.call-update) | async-done | bytes 65552 | tf_op jit(solution)/shard_map/reduce_scatter | solution.py:104
  551.0 13.7 %collective-permute-start.1 = (bf16[2,128]{1,0:T(2,128)(2,1)S(1)}, bf16[2,128]{1,0:T(2,128)(2,1)S(1)}, u32[]{:S(2)}, u32[]{:S(2)}) collective-permute-start(bf16[2,128]{1,0:T(2,128)(2,1)S(1)} %pad_maximum_fusion.8), channel_id=1, source_target_pairs={{8,0},{16,8},{24,16},{32,24},{40,32},{48,40},{56,48},{64,56},{72,6... | collective-permute-start | bytes 1544 | tf_op jit(solution)/shard_map/ppermute | solution.py:13
  567.1 4.1 all-to-all-start.7
  571.2 128.4 %all-reduce = (f32[3,128]{1,0:T(4,128)}, f32[3,128]{1,0:T(4,128)}) all-reduce(f32[3,128]{1,0:T(4,128)S(1)} %get-tuple-element.44, f32[3,128]{1,0:T(4,128)S(1)} %get-tuple-element.45), channel_id=1, replica_groups=mesh['ctx'=64,'head'=8] {'ctx'}, use_global_device_ids=true, to_apply=%region_7.0 | all-reduce | flops 768 | bytes 6144 | tf_op jit(solution)/shard_map/psum | solution.py:124
  700.3 5.4 all-to-all-start.6
  706.3 4.5 all-to-all-done.6
  (77 shorter events, 24.2 us)
Async XLA Ops:
  7.2 0.8 copy-start
  8.7 11.0 %all-to-all-start = ((bf16[32,8,128]{2,0,1:T(8,128)(2,1)}), bf16[32,8,128]{2,0,1:T(8,128)(2,1)S(1)}, u32[]{:S(2)}, u32[]{:S(2)}) async-start(bf16[32,8,128]{2,0,1:T(8,128)(2,1)} %copy_bitcast_fusion.7), calls=%async_computation | async-start | bytes 131072 | tf_op jit(solution)/shard_map/all_to_all | solution.py:53
  19.6 8.4 %all-to-all-start.1 = ((bf16[32,8,128]{2,0,1:T(8,128)(2,1)}), bf16[32,8,128]{2,0,1:T(8,128)(2,1)S(1)}, u32[]{:S(2)}, u32[]{:S(2)}) async-start(bf16[32,8,128]{2,0,1:T(8,128)(2,1)} %copy_bitcast_fusion.6), calls=%async_computation.1 | async-start | bytes 131072 | tf_op jit(solution)/shard_map/all_to_all | solution.py:54
  23.0 158.6 %all-gather.5.cloned.1.call-start = ((), (), s32[]{:S(2)}) async-start(), calls=%async_computation.10 | async-start | bytes 1064960 | tf_op jit(solution)/shard_map/all_gather | solution.py:65
  28.0 8.5 %collective-permute-start = (bf16[2,128]{1,0:T(2,128)(2,1)S(1)}, bf16[2,128]{1,0:T(2,128)(2,1)S(1)}, u32[]{:S(2)}, u32[]{:S(2)}) collective-permute-start(bf16[2,128]{1,0:T(2,128)(2,1)S(1)} %pad_maximum_fusion.7), channel_id=1, source_target_pairs={{0,8},{8,16},{16,24},{24,32},{32,40},{40,48},{48,56},{56,64},{64,7... | collective-permute-start | bytes 1544 | tf_op jit(solution)/shard_map/ppermute | solution.py:13
  36.5 151.9 %copy-start.5 = (f32[1,128]{1,0:T(1,128)}, f32[1,128]{1,0:T(1,128)S(1)}, u32[]{:S(2)}) copy-start(f32[1,128]{1,0:T(1,128)S(1)} %get-tuple-element.37) | copy-start | bytes 1540
  38.7 8.4 %all-to-all-start.2 = ((bf16[32,8,128]{2,0,1:T(8,128)(2,1)}), bf16[32,8,128]{2,0,1:T(8,128)(2,1)S(1)}, u32[]{:S(2)}, u32[]{:S(2)}) async-start(bf16[32,8,128]{2,0,1:T(8,128)(2,1)} %copy_bitcast_fusion.5), calls=%async_computation.2 | async-start | bytes 131072 | tf_op jit(solution)/shard_map/all_to_all | solution.py:52
  47.1 8.4 %all-to-all-start.4 = ((bf16[32,8,128]{2,0,1:T(8,128)(2,1)}), bf16[32,8,128]{2,0,1:T(8,128)(2,1)S(1)}, u32[]{:S(2)}, u32[]{:S(2)}) async-start(bf16[32,8,128]{2,0,1:T(8,128)(2,1)} %copy_bitcast_fusion.4), calls=%async_computation.4 | async-start | bytes 131072 | tf_op jit(solution)/shard_map/all_to_all | solution.py:55
  50.4 271.7 %all-gather.3.cloned.1.call-start = ((), (), s32[]{:S(2)}) async-start(), calls=%async_computation.9 | async-start | bytes 1064960 | tf_op jit(solution)/shard_map/all_gather | solution.py:66
  51.3 137.2 %copy-start.7 = (f32[128]{0:T(128)}, f32[128]{0:T(128)S(1)}, u32[]{:S(2)}) copy-start(f32[128]{0:T(128)S(1)} %get-tuple-element.30) | copy-start | bytes 1540
  51.3 137.2 %copy-start.9 = (f32[128]{0:T(128)}, f32[128]{0:T(128)S(1)}, u32[]{:S(2)}) copy-start(f32[128]{0:T(128)S(1)} %get-tuple-element.31) | copy-start | bytes 1540
  51.3 137.2 %copy-start.11 = (f32[128]{0:T(128)}, f32[128]{0:T(128)S(1)}, u32[]{:S(2)}) copy-start(f32[128]{0:T(128)S(1)} %get-tuple-element.29) | copy-start | bytes 1540
  56.4 493.9 %reduce-scatter.2.cloned.1.call-start = ((), (), s32[]{:S(2)}) async-start(), calls=%async_computation.11 | async-start | bytes 4259840 | tf_op jit(solution)/shard_map/reduce_scatter | solution.py:104
  192.5 1.9 copy-start.1
  323.6 3.5 copy-start.2
  328.5 1.9 copy-start.3
  330.5 5.7 copy-start.4
  342.5 222.1 %copy-start.12 = (f32[128]{0:T(128)S(1)}, f32[128]{0:T(128)}, u32[]{:S(2)}) copy-start(f32[128]{0:T(128)} %copy-done.11) | copy-start | bytes 1540
  342.5 222.9 %copy-start.6 = (f32[1,128]{1,0:T(1,128)S(1)}, f32[1,128]{1,0:T(1,128)}, u32[]{:S(2)}) copy-start(f32[1,128]{1,0:T(1,128)} %copy-done.5) | copy-start | bytes 1540
  342.5 222.9 %copy-start.8 = (f32[128]{0:T(128)S(1)}, f32[128]{0:T(128)}, u32[]{:S(2)}) copy-start(f32[128]{0:T(128)} %copy-done.7) | copy-start | bytes 1540
  342.6 222.9 %copy-start.10 = (f32[128]{0:T(128)S(1)}, f32[128]{0:T(128)}, u32[]{:S(2)}) copy-start(f32[128]{0:T(128)} %copy-done.9) | copy-start | bytes 1540
  346.4 9.1 %all-to-all-start.5 = ((bf16[8,32,128]{2,1,0:T(8,128)(2,1)}), bf16[8,32,128]{2,1,0:T(8,128)(2,1)S(1)}, u32[]{:S(2)}, u32[]{:S(2)}) async-start(bf16[8,32,128]{2,1,0:T(8,128)(2,1)} %all_to_all.122), calls=%async_computation.5 | async-start | bytes 131072 | tf_op jit(solution)/shard_map/all_to_all | solution.py:126
  355.6 8.4 %all-to-all-start.3 = ((bf16[8,32,128]{2,1,0:T(8,128)(2,1)}), bf16[8,32,128]{2,1,0:T(8,128)(2,1)S(1)}, u32[]{:S(2)}, u32[]{:S(2)}) async-start(bf16[8,32,128]{2,1,0:T(8,128)(2,1)} %all_to_all.115), calls=%async_computation.3 | async-start | bytes 131072 | tf_op jit(solution)/shard_map/all_to_all | solution.py:84
  551.0 15.4 %collective-permute-start.1 = (bf16[2,128]{1,0:T(2,128)(2,1)S(1)}, bf16[2,128]{1,0:T(2,128)(2,1)S(1)}, u32[]{:S(2)}, u32[]{:S(2)}) collective-permute-start(bf16[2,128]{1,0:T(2,128)(2,1)S(1)} %pad_maximum_fusion.8), channel_id=1, source_target_pairs={{8,0},{16,8},{24,16},{32,24},{40,32},{48,40},{56,48},{64,56},{72,6... | collective-permute-start | bytes 1544 | tf_op jit(solution)/shard_map/ppermute | solution.py:13
  567.1 133.2 %all-to-all-start.7 = ((bf16[8,32,128]{2,1,0:T(8,128)(2,1)}), bf16[8,32,128]{2,1,0:T(8,128)(2,1)S(1)}, u32[]{:S(2)}, u32[]{:S(2)}) async-start(bf16[8,32,128]{2,1,0:T(8,128)(2,1)} %bitcast.45), calls=%async_computation.8 | async-start | bytes 131072 | tf_op jit(solution)/shard_map/all_to_all | solution.py:128
  700.3 10.5 %all-to-all-start.6 = ((bf16[8,32,128]{2,1,0:T(8,128)(2,1)}), bf16[8,32,128]{2,1,0:T(8,128)(2,1)S(1)}, u32[]{:S(2)}, u32[]{:S(2)}) async-start(bf16[8,32,128]{2,1,0:T(8,128)(2,1)} %bitcast.40), calls=%async_computation.7 | async-start | bytes 131072 | tf_op jit(solution)/shard_map/all_to_all | solution.py:127
Sparse Core Ops, SparseCore 0:
  37.3 144.1 all-gather.4
  185.4 136.6 all-gather.2
  342.6 207.5 reduce-scatter.1
where the time goes:
time: 724 us; the launch traced here: 718 us
  waiting for transfers between devices  466 us (64%)
  blocking collectives  128 us (18%)
  starting transfers between devices  53.3 us (7%)
  local copies, waits for them, and re-layouts  25.7 us (4%)
  matrix products  18.5 us (3%)
  between operations  14.1 us (2%)
  other arithmetic  12.3 us (2%)
    reduce_scatter x1, waiting for transfers between devices, local(): lax.psum_scatter(jnp.concatenate([key_part.reshape(number, channels), val...  186 us
    psum x1, blocking collectives, local(): lax.psum((key_tap_terms, value_tap_terms), 'ctx')  128 us
    all_gather x1, waiting for transfers between devices, local(): lax.all_gather(key_comp, 'ctx', axis=0, tiled=True)  125 us
    all_gather x1, waiting for transfers between devices, local(): lax.all_gather(value_comp, 'ctx', axis=0, tiled=True)  125 us
    ppermute x2, starting transfers between devices, from_behind(): return lax.ppermute(array, axis, pairs)  20.4 us
  transfers between devices with their start and end apart: 13, of which 11 were waited for; matrix products, arithmetic and copies ran while one was open for 4% of the time, Pallas kernels for 0%

commit v1 on v0

v1 whole, which is shorter than its diff:
```python
import functools

import jax
import jax.numpy as jnp
from jax import lax
from jax.experimental import pallas as pl
from jax.experimental.pallas import tpu as pltpu
from jax.sharding import PartitionSpec as P

D = 1024
HEADS = 16
MESH = pl.DeviceIdType.MESH
F32 = jnp.float32
BF16 = jnp.bfloat16


def place(nz):
    ctx = lax.axis_index("ctx")
    head = lax.axis_index("head")
    core = ctx % 2
    z = (ctx // 2) % nz
    y = ctx // (2 * nz)
    return ctx, head, y, z, core


def ctx_of(nz, y, z, core):
    return (y * nz + z) * 2 + core


def remote(src, dst, send, recv, ctx, head):
    return pltpu.make_async_remote_copy(
        src_ref=src, dst_ref=dst, send_sem=send, recv_sem=recv,
        device_id={"ctx": ctx, "head": head}, device_id_type=MESH,
    )


def greet(sem, ctx, head):
    pl.semaphore_signal(sem, inc=1, device_id={"ctx": ctx, "head": head}, device_id_type=MESH)


def col(h, width):
    return pl.ds(pl.multiple_of(h * width, width), width)


def gather_kernel(nz, nh, q_in, k_in, v_in, cot_in, kt, vt,
                  q_out, cot_out, kf, vf, kv,
                  k_loc, v_loc, halo,
                  a_send, a_recv, a_self, h_send, h_recv,
                  y_send, y_recv, r_send, r_recv, l_send, l_recv, c_send, c_recv):
    ctx, head, y, z, core = place(nz)
    nctx = 4 * nz
    rows = q_in.shape[0]
    ch = q_out.shape[1]
    zr, zl = (z + 1) % nz, (z + nz - 1) % nz
    right, left = ctx_of(nz, y, zr, core), ctx_of(nz, y, zl, core)
    across = ctx_of(nz, 1 - y, z, core)
    mate = ctx_of(nz, y, z, 1 - core)
    last = nh - 1
    gives = (head == last) & (ctx < nctx - 1)
    takes = ctx >= 1

    barrier = pltpu.get_barrier_semaphore()
    for p in range(1, nh):
        greet(barrier, ctx, (head + p) % nh)
    for other in (right, left, across, mate):
        greet(barrier, other, head)

    @pl.when(takes)
    def _():
        greet(barrier, ctx - 1, last)

    @pl.when(gives)
    def _():
        pl.semaphore_wait(barrier, nh - 1 + 4 + nh)

    @pl.when(jnp.logical_not(gives))
    def _():
        pl.semaphore_wait(barrier, nh - 1 + 4)

    pairs = ((k_in, k_loc), (v_in, v_loc), (q_in, q_out), (cot_in, cot_out))

    def halo_copies():
        out = []
        for a in range(2):
            for t in range(nh):
                out.append(remote(
                    pairs[a][0].at[pl.ds(rows - 16, 16), pl.ds(t * ch, ch)], halo.at[a],
                    h_send.at[a, t], h_recv.at[a], ctx + 1, t))
        return out

    def swaps(a):
        out = []
        for p in range(1, nh):
            t = (head + p) % nh
            out.append(remote(
                pairs[a][0].at[:, col(t, ch)], pairs[a][1].at[col(head, rows), :],
                a_send.at[a, p - 1], a_recv.at[a, p - 1], ctx, t))
        return out

    def own(a):
        return pltpu.make_async_copy(
            pairs[a][0].at[:, col(head, ch)], pairs[a][1].at[col(head, rows), :], a_self.at[a])

    moves = [swaps(a) for a in range(4)]
    for a in range(2):
        own(a).start()
        for m in moves[a]:
            m.start()

    @pl.when(gives)
    def _():
        for m in halo_copies():
            m.start()

    for a in range(2, 4):
        own(a).start()
        for m in moves[a]:
            m.start()

    @pl.when(jnp.logical_not(takes))
    def _():
        kf[0:8, :] = jnp.zeros((8, ch), F32)
        vf[0:8, :] = jnp.zeros((8, ch), F32)

    @pl.when(takes)
    def _():
        for a, f in ((0, kf), (1, vf)):
            pltpu.make_async_copy(halo.at[a], halo.at[a], h_recv.at[a]).wait()
            f[0:8, :] = halo[a].astype(F32)[8:16, :]

    count = nh * rows // 4
    mine = kv.at[core, z]
    for a, f, taps in ((0, kf, kt), (1, vf, vt)):
        own(a).wait()
        for m in moves[a]:
            m.wait_recv()
        f[pl.ds(8, nh * rows), :] = pairs[a][1][...].astype(F32)
        packed = (taps[0:1, :] * f[pl.ds(7, count, stride=4), :]
                  + taps[1:2, :] * f[pl.ds(8, count, stride=4), :]
                  + taps[2:3, :] * f[pl.ds(9, count, stride=4), :])
        kv[core, z, pl.ds(pl.multiple_of(y * count, count), count), a * ch:(a + 1) * ch] = packed.astype(BF16)

    half = mine.at[pl.ds(pl.multiple_of(y * count, count), count), :]
    step_y = remote(half, half, y_send, y_recv, across, head)
    step_y.start()
    step_y.wait_recv()

    def chunk(zz):
        return kv.at[core, zz]

    def to_mate(zz, n):
        return remote(chunk(zz), chunk(zz), c_send.at[n], c_recv.at[n], mate, head)

    def to_right(s):
        zz = (z + nz - s) % nz
        return remote(chunk(zz), chunk(zz), r_send.at[s], r_recv.at[s], right, head)

    def to_left(s):
        zz = (z + s) % nz
        return remote(chunk(zz), chunk(zz), l_send.at[s], l_recv.at[s], left, head)

    nr, nl = nz // 2, nz // 2 - 1
    mates = []
    for s in range(nr):
        to_right(s).start()
        if s < nl:
            to_left(s).start()
        if s == 0:
            mates.append(to_mate(z, 0))
            mates[-1].start()
        to_right(s).wait_recv()
        if s < nl:
            to_left(s).wait_recv()
        mates.append(to_mate((z + nz - s - 1) % nz, 1 + s))
        mates[-1].start()
        if s < nl:
            mates.append(to_mate((z + s + 1) % nz, 1 + nr + s))
            mates[-1].start()
    for a in range(2, 4):
        own(a).wait()
        for m in moves[a]:
            m.wait_recv()
    for m in mates:
        m.wait()
    for s in range(nr):
        to_right(s).wait_send()
    for s in range(nl):
        to_left(s).wait_send()
    step_y.wait_send()
    for a in range(4):
        for m in moves[a]:
            m.wait_send()

    @pl.when(gives)
    def _():
        for m in halo_copies():
            m.wait_send()


def gather(nz, nh, q, k, v, cot, kt, vt):
    rows, width = q.shape
    ch = width // nh
    length = nh * rows
    count = length // 4
    vm = pl.BlockSpec(memory_space=pltpu.VMEM)
    dma = pltpu.SemaphoreType.DMA
    return pl.pallas_call(
        functools.partial(gather_kernel, nz, nh),
        out_shape=(
            jax.ShapeDtypeStruct((length, ch), BF16),
            jax.ShapeDtypeStruct((length, ch), BF16),
            jax.ShapeDtypeStruct((length + 8, ch), F32),
            jax.ShapeDtypeStruct((length + 8, ch), F32),
            jax.ShapeDtypeStruct((2, nz, 2 * count, 2 * ch), BF16),
        ),
        in_specs=[vm] * 6,
        out_specs=(vm,) * 5,
        scratch_shapes=[
            pltpu.VMEM((length, ch), BF16),
            pltpu.VMEM((length, ch), BF16),
            pltpu.VMEM((2, 16, ch), BF16),
            dma((4, nh - 1)), dma((4, nh - 1)), dma((4,)),
            dma((2, nh)), dma((2,)),
            dma(()), dma(()),
            dma((nz // 2,)), dma((nz // 2,)),
            dma((nz // 2,)), dma((nz // 2,)),
            dma((nz,)), dma((nz,)),
        ],
        compiler_params=pltpu.CompilerParams(
            collective_id=0, has_side_effects=True, vmem_limit_bytes=40 << 20),
        name="gather",
    )(q, k, v, cot, kt, vt)


def scatter_kernel(nz, nh, part, att_in, gq_in, kf, vf, kt, vt,
                   att_out, gq_out, gk_out, gv_out, kt_out, vt_out,
                   pin, rbuf, rout, lbuf, lout, ybuf, yout, spread, gk_loc, gv_loc,
                   edge, edge_in, tap1, tap2,
                   a_send, a_recv, a_self, e_send, e_recv,
                   y_send, y_recv, r_send, r_recv, l_send, l_recv, c_send, c_recv,
                   t_send, t_recv, u_send, u_recv):
    ctx, head, y, z, core = place(nz)
    nctx = 4 * nz
    rows = att_out.shape[0]
    ch = att_in.shape[1]
    count = nh * rows // 4
    zr, zl = (z + 1) % nz, (z + nz - 1) % nz
    right, left = ctx_of(nz, y, zr, core), ctx_of(nz, y, zl, core)
    across = ctx_of(nz, 1 - y, z, core)
    mate = ctx_of(nz, y, z, 1 - core)
    corner = ctx_of(nz, 1 - y, z, 1 - core)
    last = nh - 1
    takes = (head == last) & (ctx < nctx - 1)
    gives = ctx >= 1

    barrier = pltpu.get_barrier_semaphore()
    for p in range(1, nh):
        greet(barrier, ctx, (head + p) % nh)
    for p in range(1, nz):
        greet(barrier, ctx_of(nz, y, (z + p) % nz, core), head)
    for other in (across, mate, corner):
        greet(barrier, other, head)

    @pl.when(takes)
    def _():
        for t in range(nh):
            greet(barrier, ctx + 1, t)

    @pl.when(gives)
    def _():
        pl.semaphore_wait(barrier, nh - 1 + nz - 1 + 3 + 1)

    @pl.when(jnp.logical_not(gives))
    def _():
        pl.semaphore_wait(barrier, nh - 1 + nz - 1 + 3)

    nr, nl = nz // 2, nz // 2 - 1

    def to_mate(zz, n):
        return remote(part.at[1 - core, zz], pin.at[zz], c_send.at[n], c_recv.at[n], mate, head)

    order = []
    for s in range(nr):
        order.append((z + nz // 2 + nz - s) % nz)
        if s < nl:
            order.append((z + nz - nl + s) % nz)
    order.append(z)
    mates = [to_mate(zz, n) for n, zz in enumerate(order)]
    for m in mates:
        m.start()

    pairs = ((att_in, att_out), (gq_in, gq_out), (gk_loc, gk_out), (gv_loc, gv_out))

    def swaps(a):
        out = []
        for p in range(1, nh):
            t = (head + p) % nh
            out.append(remote(
                pairs[a][0].at[col(t, rows), :], pairs[a][1].at[:, col(head, ch)],
                a_send.at[a, p - 1], a_recv.at[a, p - 1], ctx, t))
        return out

    def own(a):
        return pltpu.make_async_copy(
            pairs[a][0].at[col(head, rows), :], pairs[a][1].at[:, col(head, ch)], a_self.at[a])

    moves = [swaps(a) for a in range(4)]
    for a in range(2):
        own(a).start()
        for m in moves[a]:
            m.start()

    def local_sum(n):
        mates[n].wait_recv()
        zz = order[n]
        return part[core, zz].astype(F32) + pin[zz].astype(F32)

    def to_right(s):
        return remote(rout.at[s], rbuf.at[s], r_send.at[s], r_recv.at[s], right, head)

    def to_left(s):
        return remote(lout.at[s], lbuf.at[s], l_send.at[s], l_recv.at[s], left, head)

    n = 0
    for s in range(nr):
        total = local_sum(n)
        n += 1
        if s > 0:
            to_right(s - 1).wait_recv()
            total = total + rbuf[s - 1].astype(F32)
        rout[s] = total.astype(BF16)
        to_right(s).start()
        if s < nl:
            total = local_sum(n)
            n += 1
            if s > 0:
                to_left(s - 1).wait_recv()
                total = total + lbuf[s - 1].astype(F32)
            lout[s] = total.astype(BF16)
            to_left(s).start()
    total = local_sum(n)
    to_left(nl - 1).wait_recv()
    total = total + lbuf[nl - 1].astype(F32)
    to_right(nr - 1).wait_recv()
    rout[nr] = (total + rbuf[nr - 1].astype(F32)).astype(BF16)
    ybuf[...] = total + rbuf[nr - 1].astype(F32)
    theirs = rout.at[nr, pl.ds(pl.multiple_of((1 - y) * count, count), count), :]
    step_y = remote(theirs, yout, y_send, y_recv, across, head)
    step_y.start()
    step_y.wait_recv()
    grads = ybuf[pl.ds(pl.multiple_of(y * count, count), count), :] + yout[...].astype(F32)

    tap1[z, 6:8, :] = jnp.zeros((2, ch), F32)
    for a, f, taps, loc in ((0, kf, kt, gk_loc), (1, vf, vt, gv_loc)):
        g = grads[:, a * ch:(a + 1) * ch]
        spread[a, 0:8, :] = jnp.zeros((8, ch), F32)
        spread[a, pl.ds(nh * rows, 8), :] = jnp.zeros((8, ch), F32)
        spread[a, pl.ds(7, count, stride=4), :] = taps[0:1, :] * g
        spread[a, pl.ds(8, count, stride=4), :] = taps[1:2, :] * g
        spread[a, pl.ds(9, count, stride=4), :] = taps[2:3, :] * g
        spread[a, pl.ds(10, count, stride=4), :] = jnp.zeros((count, ch), F32)
        spread[a, pl.ds(nh * rows + 7, 1), :] = jnp.zeros((1, ch), F32)
        loc[...] = spread[a, pl.ds(8, nh * rows), :].astype(BF16)
        edge[a] = jnp.concatenate([jnp.zeros((8, ch), F32), spread[a, 0:8, :]], axis=0).astype(BF16)
        for t in range(3):
            tap1[z, 3 * a + t:3 * a + t + 1, :] = jnp.sum(
                g * f[pl.ds(7 + t, count, stride=4), :], axis=0, keepdims=True)

    def tap_z():
        out = []
        for p in range(1, nz):
            out.append(remote(tap1.at[z], tap1.at[z], t_send.at[p - 1], t_recv.at[p - 1],
                              ctx_of(nz, y, (z + p) % nz, core), head))
        return out

    def tap_yc():
        out = []
        for m, other in enumerate((across, mate, corner)):
            spot = tap2.at[2 * y + core]
            out.append(remote(spot, spot, u_send.at[m], u_recv.at[m], other, head))
        return out

    def edges():
        return [remote(edge.at[a], edge_in.at[a, head], e_send.at[a], e_recv.at[a, head],
                       ctx - 1, last) for a in range(2)]

    for m in tap_z():
        m.start()

    @pl.when(gives)
    def _():
        for m in edges():
            m.start()

    for a in range(2, 4):
        own(a).start()
        for m in moves[a]:
            m.start()

    for m in tap_z():
        m.wait_recv()
    total = tap1[0]
    for i in range(1, nz):
        total = total + tap1[i]
    tap2[2 * y + core] = total
    for m in tap_yc():
        m.start()

    for a in range(4):
        own(a).wait()
        for m in moves[a]:
            m.wait_recv()

    @pl.when(takes)
    def _():
        for a in range(2):
            for t in range(nh):
                pltpu.make_async_copy(edge_in.at[a, t], edge_in.at[a, t], e_recv.at[a, t]).wait()
                spot = (pl.ds(rows - 16, 16), pl.ds(t * ch, ch))
                out = pairs[2 + a][1]
                out[spot] = (out[spot].astype(F32) + edge_in[a, t].astype(F32)).astype(BF16)

    for m in tap_yc():
        m.wait_recv()
    total = (tap2[0] + tap2[1]) + (tap2[2] + tap2[3])
    kt_out[...] = total[0:3, :]
    vt_out[...] = total[3:6, :]

    for m in mates:
        m.wait_send()
    for s in range(nr):
        to_right(s).wait_send()
    for s in range(nl):
        to_left(s).wait_send()
    step_y.wait_send()
    for a in range(4):
        for m in moves[a]:
            m.wait_send()
    for m in tap_z():
        m.wait_send()
    for m in tap_yc():
        m.wait_send()

    @pl.when(gives)
    def _():
        for m in edges():
            m.wait_send()


def scatter(nz, nh, part, att, gq, kf, vf, kt, vt):
    length, ch = att.shape
    rows = length // nh
    count = length // 4
    vm = pl.BlockSpec(memory_space=pltpu.VMEM)
    dma = pltpu.SemaphoreType.DMA
    nr, nl = nz // 2, nz // 2 - 1
    wide = jax.ShapeDtypeStruct((rows, nh * ch), BF16)
    small = jax.ShapeDtypeStruct((3, ch), F32)
    return pl.pallas_call(
        functools.partial(scatter_kernel, nz, nh),
        out_shape=(wide, wide, wide, wide, small, small),
        in_specs=[vm] * 7,
        out_specs=(vm,) * 6,
        scratch_shapes=[
            pltpu.VMEM((nz, 2 * count, 2 * ch), BF16),
            pltpu.VMEM((nr, 2 * count, 2 * ch), BF16),
            pltpu.VMEM((nr + 1, 2 * count, 2 * ch), BF16),
            pltpu.VMEM((nl, 2 * count, 2 * ch), BF16),
            pltpu.VMEM((nl, 2 * count, 2 * ch), BF16),
            pltpu.VMEM((2 * count, 2 * ch), F32),
            pltpu.VMEM((count, 2 * ch), BF16),
            pltpu.VMEM((2, length + 16, ch), F32),
            pltpu.VMEM((length, ch), BF16),
            pltpu.VMEM((length, ch), BF16),
            pltpu.VMEM((2, 16, ch), BF16),
            pltpu.VMEM((2, nh, 16, ch), BF16),
            pltpu.VMEM((nz, 8, ch), F32),
            pltpu.VMEM((4, 8, ch), F32),
            dma((4, nh - 1)), dma((4, nh - 1)), dma((4,)),
            dma((2,)), dma((2, nh)),
            dma(()), dma(()),
            dma((nr,)), dma((nr,)),
            dma((nl,)), dma((nl,)),
            dma((nz,)), dma((nz,)),
            dma((nz - 1,)), dma((nz - 1,)),
            dma((3,)), dma((3,)),
        ],
        compiler_params=pltpu.CompilerParams(
            collective_id=1, has_side_effects=True, vmem_limit_bytes=40 << 20),
        name="scatter",
    )(part, att, gq, kf, vf, kt, vt)


def attention(q, cot, kv):
    length, channels = q.shape
    head_dim = D // HEADS
    heads = channels // head_dim
    scaling = head_dim ** (-0.5)
    flat = kv.reshape(-1, 2 * channels)
    qh = q.reshape(length, heads, head_dim)
    ch = cot.reshape(length, heads, head_dim)
    kh = flat[:, :channels].reshape(-1, heads, head_dim)
    vh = flat[:, channels:].reshape(-1, heads, head_dim)
    scores = jnp.einsum("qhd,khd->hqk", qh, kh, preferred_element_type=F32) * scaling
    raised = jnp.exp(scores - jnp.max(scores, axis=2, keepdims=True))
    weights = (raised / jnp.sum(raised, axis=2, keepdims=True)).astype(BF16)
    att = jnp.einsum("hqk,khd->qhd", weights, vh, preferred_element_type=F32).astype(BF16)
    offset = jnp.sum(ch.astype(F32) * att.astype(F32), axis=2)
    dweights = jnp.einsum("qhd,khd->hqk", ch, vh, preferred_element_type=F32)
    dscores = (weights.astype(F32) * (dweights - offset.T[:, :, None])).astype(BF16)
    gq = (jnp.einsum("hqk,khd->qhd", dscores, kh, preferred_element_type=F32) * scaling).astype(BF16)
    gk = jnp.einsum("hqk,qhd->khd", dscores, qh, preferred_element_type=F32) * scaling
    gv = jnp.einsum("hqk,qhd->khd", weights, ch, preferred_element_type=F32)
    part = jnp.concatenate(
        [gk.reshape(-1, channels), gv.reshape(-1, channels)], axis=1).astype(BF16)
    return att.reshape(length, channels), gq.reshape(length, channels), part.reshape(kv.shape)


def local(query_rows, key_rows, value_rows, cotangent, key_taps, value_taps):
    nz = lax.axis_size("ctx") // 4
    nh = lax.axis_size("head")
    q, cot, kf, vf, kv = gather(
        nz, nh, query_rows, key_rows, value_rows, cotangent, key_taps, value_taps)
    att, gq, part = attention(q, cot, kv)
    return scatter(nz, nh, part, att, gq, kf, vf, key_taps, value_taps)


def solution(mesh):
    rows = P(("ctx", "head"), None)
    taps = P(None, "head")
    return jax.shard_map(
        local,
        mesh=mesh,
        in_specs=(rows, rows, rows, rows, taps, taps),
        out_specs=(rows, rows, rows, rows, taps, taps),
        check_vma=False,
    )
```

time: 724 us -> 149 us (0.21)
  waiting for transfers between devices: 466 us -> 0 us
  blocking collectives: 128 us -> 0 us
  Pallas kernels: 0 us -> 111 us
  starting transfers between devices: 53.3 us -> 0 us
  between operations: 14.1 us -> 0.84 us
  local copies, waits for them, and re-layouts: 25.7 us -> 17.9 us
    all_gather x2 -> x0, waiting for transfers between devices: 250 us -> none  [the longest x1 125 us: local(): lax.all_gather(key_comp, 'ctx', axis=0, tiled=True)]
    reduce_scatter x1 -> x0, waiting for transfers between devices: 186 us -> none  [local(): lax.psum_scatter(jnp.concatenate([key_part.reshape(number, channels), val...]
    psum x1 -> x0, blocking collectives: 128 us -> none  [local(): lax.psum((key_tap_terms, value_tap_terms), 'ctx')]
    pallas_call x0 -> x2, Pallas kernels: none -> 111 us  [the longest x1 56.8 us: gather(): pl.pallas_call(functools.partial(gather_kernel, nz, nh), out_shape=(jax.S...]
    all_to_all x8 -> x0, starting transfers between devices: 32.8 us -> none  [the longest x1 5.85 us: local(): lax.all_to_all(key_rows, 'head', split_axis=1, concat_axis=0, tiled=True)]
    all_to_all x8 -> x0, waiting for transfers between devices: 28.3 us -> none  [the longest x1 4.48 us: local(): lax.all_to_all(grad_key_loc, 'head', split_axis=0, concat_axis=1, tiled=T...]
    ppermute x2 -> x0, starting transfers between devices: 20.4 us -> none  [from_behind(): return lax.ppermute(array, axis, pairs)]
    all_to_all x10 -> x0, local copies, waits for them, and re-layouts: 9.12 us -> none  [the longest x1 1.48 us: local(): lax.all_to_all(query_rows, 'head', split_axis=1, concat_axis=0, tiled=True)]
  transfers between devices with their start and end apart: 13 -> 0, of which waited for: 11 -> 0; matrix products, arithmetic and copies ran while one was open for 4% -> 0% of each run, Pallas kernels for 0% -> 0%
where the time goes in v1:
time: 149 us
  Pallas kernels  111 us (74%)
  local copies, waits for them, and re-layouts  17.9 us (12%)
  matrix products  13.2 us (9%)
  other arithmetic  6.1 us (4%)
    pallas_call x1, Pallas kernels, gather(): pl.pallas_call(functools.partial(gather_kernel, nz, nh), out_shape=(jax.S...  56.8 us
    pallas_call x1, Pallas kernels, scatter(): pl.pallas_call(functools.partial(scatter_kernel, nz, nh), out_shape=(wide...  53.9 us
    unnamed x32, local copies, waits for them, and re-layouts  9.66 us
    sub x1, matrix products, attention(): raised = jnp.exp(scores - jnp.max(scores, axis=2, keepdims=True))  5 us
    convert_element_type x1, other arithmetic, attention(): weights = (raised / jnp.sum(raised, axis=2, keepdims=True)).astype(BF16)  4.62 us
    dot_general x1, matrix products, attention(): gv = jnp.einsum('hqk,qhd->khd', weights, ch, preferred_element_type=F32)  3.19 us
    slice x2, local copies, waits for them, and re-layouts, attention(): vh = flat[:, channels:].reshape(-1, heads, head_dim)  2.99 us

profile of v1, /device:TPU:1, one launch (start us, length us, event | category | flops | bytes accessed | tf_op | source)
XLA Modules:
  0.0 148.7 jit_solution(14996851575206373176)
XLA Ops:
  0.6 0.8 copy-done
  1.5 0.8 copy-done.1
  2.3 0.8 copy-done.2
  3.2 0.8 copy-done.3
  4.0 0.7 copy-done.4
  4.7 0.7 copy-done.6
  5.4 56.8 %gather.1 = (bf16[256,128]{1,0:T(8,128)(2,1)S(1)}, bf16[256,128]{1,0:T(8,128)(2,1)S(1)}, f32[264,128]{1,0:T(8,128)S(1)}, f32[264,128]{1,0:T(8,128)S(1)}, bf16[2,16,128,256]{3,2,1,0:T(8,128)(2,1)S(1)}) custom-call(bf16[32,1024]{1,0:T(8,128)(2,1)S(1)} %copy-done, bf16[32,1024]{1,0:T(8,128)(2,1)S(1)} %copy-done.1, bf16[32,1024]{1,0:T(8,128)(2,1)S(1)} %copy-done.2, ...), custom_call_target="tpu_custom_call" | custom-call | tf_op jit(solution)/shard_map/gather/pallas_call | solution.py:207
  62.1 0.7 copy.23
  62.9 1.5 fusion.8
  64.4 1.5 %copy.26 = bf16[4096,128]{0,1:T(8,128)(2,1)S(1)} copy(bf16[4096,128]{1,0:T(8,128)(2,1)} %get-tuple-element.16) | data formatting | bytes 2097152 | tf_op jit(solution)/shard_map/slice | solution.py:503
  66.0 1.5 copy.24
  67.5 5.0 %fusion.9 = (f32[2,256]{1,0:T(2,128)S(1)}, f32[2,256,4096]{2,1,0:T(8,128)}) fusion(bf16[256,2,64]{0,2,1:T(8,128)(2,1)S(1)} %bitcast.52, bf16[4096,2,64]{0,2,1:T(8,128)(2,1)S(1)} %bitcast.45), kind=kOutput, calls=%fused_computation.18 | convolution fusion | flops 274731008 | bytes 9504768 | tf_op jit(solution)/shard_map/sub | solution.py:505
  72.5 4.6 %divide_convert_fusion = bf16[2,256,4096]{2,1,0:T(8,128)(2,1)S(1)} fusion(f32[2,256,4096]{2,1,0:T(8,128)} %get-tuple-element.19, f32[2,256]{1,0:T(2,128)S(1)} %get-tuple-element.18), kind=kLoop, calls=%fused_computation.2 | loop fusion | flops 4194304 | bytes 12584960 | tf_op jit(solution)/shard_map/convert_element_type | solution.py:506
  77.1 1.4 multiply_reduce_fusion.1
  78.6 0.5 copy-done.8
  79.2 3.2 %convolution_convert_fusion = bf16[2,64,4096]{2,1,0:T(8,128)(2,1)S(1)} fusion(bf16[256,2,64]{0,2,1:T(8,128)(2,1)S(1)} %bitcast.49, bf16[2,256,4096]{2,1,0:T(8,128)(2,1)} %copy-done.8), kind=kOutput, calls=%fused_computation.8 | convolution fusion | flops 268959744 | bytes 5308416 | tf_op jit(solution)/shard_map/hqk,qhd->khd/dot_general | solution.py:513
  82.4 0.3 copy-done.9
  82.6 1.3 multiply_convert_fusion
  84.0 1.4 fusion.4
  85.4 0.8 fusion.2
  86.3 0.2 copy.31
  86.5 1.7 %copy.27 = bf16[2,16,128,128]{3,2,1,0:T(8,128)(2,1)} copy(bf16[2,16,128,128]{2,1,0,3:T(8,128)(2,1)S(1)} %bitcast.43) | data formatting | bytes 2097152 | tf_op jit(solution)/shard_map/concatenate | solution.py:514
  88.4 0.2 copy.32
  88.6 1.0 copy.28
  89.6 1.5 pad_maximum_fusion.part
  91.1 53.9 %scatter.1 = (bf16[32,1024]{1,0:T(8,128)(2,1)S(1)}, bf16[32,1024]{1,0:T(8,128)(2,1)S(1)}, bf16[32,1024]{1,0:T(8,128)(2,1)S(1)}, bf16[32,1024]{1,0:T(8,128)(2,1)S...) custom-call(bf16[2,16,128,256]{3,2,1,0:T(8,128)(2,1)S(1)} %pad_maximum_fusion.part, bf16[256,128]{1,0:T(8,128)(2,1)S(1)} %copy.29.att_in, ...), custom_call_target="tpu_custom_call" | custom-call | tf_op jit(solution)/shard_map/scatter/pallas_call | solution.py:459
  145.1 0.6 copy.39
  145.7 0.6 copy.40
  146.3 0.6 copy.41
  146.9 0.6 copy.42
  147.6 0.6 copy.43
  148.2 0.6 copy.44
  (19 shorter events, 0.4 us)
Async XLA Ops:
  0.6 0.8 copy-start
  1.5 0.8 copy-start.1
  2.3 0.8 copy-start.2
  3.2 0.8 copy-start.3
  4.0 0.7 copy-start.4
  4.7 0.7 copy-start.6
  64.4 3.1 %copy-start.10 = (bf16[256,128]{0,1:T(8,128)(2,1)S(1)}, bf16[256,128]{0,1:T(8,128)(2,1)}, u32[]{:S(2)}) copy-start(bf16[256,128]{0,1:T(8,128)(2,1)} %copy.23) | copy-start | bytes 196612
  77.1 1.9 %copy-start.8 = (bf16[2,256,4096]{2,1,0:T(8,128)(2,1)}, bf16[2,256,4096]{2,1,0:T(8,128)(2,1)S(1)}, u32[]{:S(2)}) copy-start(bf16[2,256,4096]{2,1,0:T(8,128)(2,1)S(1)} %divide_convert_fusion) | copy-start | bytes 12582916
  79.2 3.5 %copy-start.9 = (bf16[2,256,4096]{2,1,0:T(8,128)(2,1)S(1)}, bf16[2,256,4096]{2,1,0:T(8,128)(2,1)}, u32[]{:S(2)}) copy-start(bf16[2,256,4096]{2,1,0:T(8,128)(2,1)} %copy-done.8) | copy-start | bytes 12582916
  84.0 1.4 copy-start.11
  88.3 2.8 %copy-start.5 = (f32[3,128]{1,0:T(4,128)S(1)}, f32[3,128]{1,0:T(4,128)}, u32[]{:S(2)}) copy-start(f32[3,128]{1,0:T(4,128)} %kt.3) | copy-start | bytes 4612
  88.3 2.8 %copy-start.7 = (f32[3,128]{1,0:T(4,128)S(1)}, f32[3,128]{1,0:T(4,128)}, u32[]{:S(2)}) copy-start(f32[3,128]{1,0:T(4,128)} %vt.3) | copy-start | bytes 4612

commit v2 on v1

--- a/solution.py
+++ b/solution.py
@@ -112,11 +112,6 @@
         for m in halo_copies():
             m.start()
 
-    for a in range(2, 4):
-        own(a).start()
-        for m in moves[a]:
-            m.start()
-
     @pl.when(jnp.logical_not(takes))
     def _():
         kf[0:8, :] = jnp.zeros((8, ch), F32)
@@ -129,7 +124,6 @@
             f[0:8, :] = halo[a].astype(F32)[8:16, :]
 
     count = nh * rows // 4
-    mine = kv.at[core, z]
     for a, f, taps in ((0, kf, kt), (1, vf, vt)):
         own(a).wait()
         for m in moves[a]:
@@ -140,52 +134,61 @@
                   + taps[2:3, :] * f[pl.ds(9, count, stride=4), :])
         kv[core, z, pl.ds(pl.multiple_of(y * count, count), count), a * ch:(a + 1) * ch] = packed.astype(BF16)
 
-    half = mine.at[pl.ds(pl.multiple_of(y * count, count), count), :]
-    step_y = remote(half, half, y_send, y_recv, across, head)
+    def chunk(zz, u):
+        side = y + u - 2 * u * y
+        return kv.at[core, zz, pl.ds(pl.multiple_of(side * count, count), count), :]
+
+    def to_mate(zz, u, n):
+        return remote(chunk(zz, u), chunk(zz, u), c_send.at[n, u], c_recv.at[n, u], mate, head)
+
+    def to_right(s, u):
+        here = chunk((z + nz - s) % nz, u)
+        return remote(here, here, r_send.at[s, u], r_recv.at[s, u], right, head)
+
+    def to_left(s, u):
+        here = chunk((z + s) % nz, u)
+        return remote(here, here, l_send.at[s, u], l_recv.at[s, u], left, head)
+
+    nr, nl = nz // 2, nz // 2 - 1
+    step_y = remote(chunk(z, 0), chunk(z, 0), y_send, y_recv, across, head)
     step_y.start()
+    to_right(0, 0).start()
+    to_left(0, 0).start()
+    mates = [to_mate(z, 0, 0)]
+    mates[0].start()
+    for a in range(2, 4):
+        own(a).start()
+        for m in moves[a]:
+            m.start()
     step_y.wait_recv()
-
-    def chunk(zz):
-        return kv.at[core, zz]
-
-    def to_mate(zz, n):
-        return remote(chunk(zz), chunk(zz), c_send.at[n], c_recv.at[n], mate, head)
-
-    def to_right(s):
-        zz = (z + nz - s) % nz
-        return remote(chunk(zz), chunk(zz), r_send.at[s], r_recv.at[s], right, head)
-
-    def to_left(s):
-        zz = (z + s) % nz
-        return remote(chunk(zz), chunk(zz), l_send.at[s], l_recv.at[s], left, head)
-
-    nr, nl = nz // 2, nz // 2 - 1
-    mates = []
+    to_right(0, 1).start()
+    to_left(0, 1).start()
+    mates.append(to_mate(z, 1, 0))
+    mates[1].start()
     for s in range(nr):
-        to_right(s).start()
-        if s < nl:
-            to_left(s).start()
-        if s == 0:
-            mates.append(to_mate(z, 0))
+        for u in range(2):
+            to_right(s, u).wait_recv()
+            if s + 1 < nr:
+                to_right(s + 1, u).start()
+            mates.append(to_mate((z + nz - s - 1) % nz, u, 1 + s))
             mates[-1].start()
-        to_right(s).wait_recv()
-        if s < nl:
-            to_left(s).wait_recv()
-        mates.append(to_mate((z + nz - s - 1) % nz, 1 + s))
-        mates[-1].start()
-        if s < nl:
-            mates.append(to_mate((z + s + 1) % nz, 1 + nr + s))
-            mates[-1].start()
+            if s < nl:
+                to_left(s, u).wait_recv()
+                if s + 1 < nl:
+                    to_left(s + 1, u).start()
+                mates.append(to_mate((z + s + 1) % nz, u, 1 + nr + s))
+                mates[-1].start()
     for a in range(2, 4):
         own(a).wait()
         for m in moves[a]:
             m.wait_recv()
     for m in mates:
         m.wait()
-    for s in range(nr):
-        to_right(s).wait_send()
-    for s in range(nl):
-        to_left(s).wait_send()
+    for u in range(2):
+        for s in range(nr):
+            to_right(s, u).wait_send()
+        for s in range(nl):
+            to_left(s, u).wait_send()
     step_y.wait_send()
     for a in range(4):
         for m in moves[a]:
@@ -213,7 +216,7 @@
             jax.ShapeDtypeStruct((length + 8, ch), F32),
             jax.ShapeDtypeStruct((2, nz, 2 * count, 2 * ch), BF16),
         ),
-        in_specs=[vm] * 6,
+        in_specs=[pl.BlockSpec(memory_space=pltpu.HBM)] * 4 + [vm] * 2,
         out_specs=(vm,) * 5,
         scratch_shapes=[
             pltpu.VMEM((length, ch), BF16),
@@ -222,9 +225,9 @@
             dma((4, nh - 1)), dma((4, nh - 1)), dma((4,)),
             dma((2, nh)), dma((2,)),
             dma(()), dma(()),
-            dma((nz // 2,)), dma((nz // 2,)),
-            dma((nz // 2,)), dma((nz // 2,)),
-            dma((nz,)), dma((nz,)),
+            dma((nz // 2, 2)), dma((nz // 2, 2)),
+            dma((nz // 2 - 1, 2)), dma((nz // 2 - 1, 2)),
+            dma((nz, 2)), dma((nz, 2)),
         ],
         compiler_params=pltpu.CompilerParams(
             collective_id=0, has_side_effects=True, vmem_limit_bytes=40 << 20),
@@ -310,45 +313,51 @@
         for m in moves[a]:
             m.start()
 
-    def local_sum(n):
-        mates[n].wait_recv()
+    def part_of(u):
+        side = 1 - y - u + 2 * u * y
+        return pl.ds(pl.multiple_of(side * count, count), count)
+
+    def local_sum(n, u):
+        if u == 0:
+            mates[n].wait_recv()
         zz = order[n]
-        return part[core, zz].astype(F32) + pin[zz].astype(F32)
-
-    def to_right(s):
-        return remote(rout.at[s], rbuf.at[s], r_send.at[s], r_recv.at[s], right, head)
-
-    def to_left(s):
-        return remote(lout.at[s], lbuf.at[s], l_send.at[s], l_recv.at[s], left, head)
-
-    n = 0
+        return part[core, zz, part_of(u), :].astype(F32) + pin[zz, part_of(u), :].astype(F32)
+
+    def to_right(s, u):
+        return remote(rout.at[s, u], rbuf.at[s, u], r_send.at[s, u], r_recv.at[s, u], right, head)
+
+    def to_left(s, u):
+        return remote(lout.at[s, u], lbuf.at[s, u], l_send.at[s, u], l_recv.at[s, u], left, head)
+
     for s in range(nr):
-        total = local_sum(n)
-        n += 1
-        if s > 0:
-            to_right(s - 1).wait_recv()
-            total = total + rbuf[s - 1].astype(F32)
-        rout[s] = total.astype(BF16)
-        to_right(s).start()
-        if s < nl:
-            total = local_sum(n)
-            n += 1
+        for u in range(2):
+            n = 2 * s
+            total = local_sum(n, u)
             if s > 0:
-                to_left(s - 1).wait_recv()
-                total = total + lbuf[s - 1].astype(F32)
-            lout[s] = total.astype(BF16)
-            to_left(s).start()
-    total = local_sum(n)
-    to_left(nl - 1).wait_recv()
-    total = total + lbuf[nl - 1].astype(F32)
-    to_right(nr - 1).wait_recv()
-    rout[nr] = (total + rbuf[nr - 1].astype(F32)).astype(BF16)
-    ybuf[...] = total + rbuf[nr - 1].astype(F32)
-    theirs = rout.at[nr, pl.ds(pl.multiple_of((1 - y) * count, count), count), :]
-    step_y = remote(theirs, yout, y_send, y_recv, across, head)
-    step_y.start()
-    step_y.wait_recv()
-    grads = ybuf[pl.ds(pl.multiple_of(y * count, count), count), :] + yout[...].astype(F32)
+                to_right(s - 1, u).wait_recv()
+                total = total + rbuf[s - 1, u].astype(F32)
+            rout[s, u] = total.astype(BF16)
+            to_right(s, u).start()
+            if s < nl:
+                total = local_sum(n + 1, u)
+                if s > 0:
+                    to_left(s - 1, u).wait_recv()
+                    total = total + lbuf[s - 1, u].astype(F32)
+                lout[s, u] = total.astype(BF16)
+                to_left(s, u).start()
+    for u in range(2):
+        total = local_sum(2 * nr - 1, u)
+        to_left(nl - 1, u).wait_recv()
+        total = total + lbuf[nl - 1, u].astype(F32)
+        to_right(nr - 1, u).wait_recv()
+        total = total + rbuf[nr - 1, u].astype(F32)
+        if u == 0:
+            ybuf[...] = total.astype(BF16)
+            step_y = remote(ybuf, yout, y_send, y_recv, across, head)
+            step_y.start()
+        else:
+            step_y.wait_recv()
+            grads = total + yout[...].astype(F32)
 
     tap1[z, 6:8, :] = jnp.zeros((2, ch), F32)
     for a, f, taps, loc in ((0, kf, kt, gk_loc), (1, vf, vt, gv_loc)):
@@ -428,10 +437,11 @@
 
     for m in mates:
         m.wait_send()
-    for s in range(nr):
-        to_right(s).wait_send()
-    for s in range(nl):
-        to_left(s).wait_send()
+    for u in range(2):
+        for s in range(nr):
+            to_right(s, u).wait_send()
+        for s in range(nl):
+            to_left(s, u).wait_send()
     step_y.wait_send()
     for a in range(4):
         for m in moves[a]:
@@ -463,11 +473,11 @@
         out_specs=(vm,) * 6,
         scratch_shapes=[
             pltpu.VMEM((nz, 2 * count, 2 * ch), BF16),
-            pltpu.VMEM((nr, 2 * count, 2 * ch), BF16),
-            pltpu.VMEM((nr + 1, 2 * count, 2 * ch), BF16),
-            pltpu.VMEM((nl, 2 * count, 2 * ch), BF16),
-            pltpu.VMEM((nl, 2 * count, 2 * ch), BF16),
-            pltpu.VMEM((2 * count, 2 * ch), F32),
+            pltpu.VMEM((nr, 2, count, 2 * ch), BF16),
+            pltpu.VMEM((nr, 2, count, 2 * ch), BF16),
+            pltpu.VMEM((nl, 2, count, 2 * ch), BF16),
+            pltpu.VMEM((nl, 2, count, 2 * ch), BF16),
+            pltpu.VMEM((count, 2 * ch), BF16),
             pltpu.VMEM((count, 2 * ch), BF16),
             pltpu.VMEM((2, length + 16, ch), F32),
             pltpu.VMEM((length, ch), BF16),
@@ -479,8 +489,8 @@
             dma((4, nh - 1)), dma((4, nh - 1)), dma((4,)),
             dma((2,)), dma((2, nh)),
             dma(()), dma(()),
-            dma((nr,)), dma((nr,)),
-            dma((nl,)), dma((nl,)),
+            dma((nr, 2)), dma((nr, 2)),
+            dma((nl, 2)), dma((nl, 2)),
             dma((nz,)), dma((nz,)),
             dma((nz - 1,)), dma((nz - 1,)),
             dma((3,)), dma((3,)),

time: 149 us -> 138 us (0.926)
  Pallas kernels: 111 us -> 99.3 us
    pallas_call x1, Pallas kernels: 53.9 us -> 47.1 us  [scatter(): pl.pallas_call(functools.partial(scatter_kernel, nz, nh), out_shape=(wide...]
    pallas_call x1, Pallas kernels: 56.8 us -> 52.2 us  [gather(): pl.pallas_call(functools.partial(gather_kernel, nz, nh), out_shape=(jax.S...]
where the time goes in v2:
time: 138 us; the launch traced here: 137 us
  Pallas kernels  99.3 us (72%)
  local copies, waits for them, and re-layouts  17.9 us (13%)
  matrix products  13.2 us (10%)
  other arithmetic  6.1 us (4%)
    pallas_call x1, Pallas kernels, gather(): pl.pallas_call(functools.partial(gather_kernel, nz, nh), out_shape=(jax.S...  52.2 us
    pallas_call x1, Pallas kernels, scatter(): pl.pallas_call(functools.partial(scatter_kernel, nz, nh), out_shape=(wide...  47.1 us
    unnamed x32, local copies, waits for them, and re-layouts  9.66 us
    sub x1, matrix products, attention(): raised = jnp.exp(scores - jnp.max(scores, axis=2, keepdims=True))  5 us
    convert_element_type x1, other arithmetic, attention(): weights = (raised / jnp.sum(raised, axis=2, keepdims=True)).astype(BF16)  4.62 us
    dot_general x1, matrix products, attention(): gv = jnp.einsum('hqk,qhd->khd', weights, ch, preferred_element_type=F32)  3.19 us
    slice x2, local copies, waits for them, and re-layouts, attention(): vh = flat[:, channels:].reshape(-1, heads, head_dim)  2.99 us

profile of v2, /device:TPU:1, one launch (start us, length us, event | category | flops | bytes accessed | tf_op | source)
XLA Modules:
  0.0 137.3 jit_solution(13887970161118694300)
XLA Ops:
  0.6 0.8 copy-done
  1.5 0.8 copy-done.1
  2.3 0.8 copy-done.2
  3.2 0.8 copy-done.3
  4.0 0.7 copy-done.4
  4.7 0.7 copy-done.6
  5.4 52.2 %gather.1 = (bf16[256,128]{1,0:T(8,128)(2,1)S(1)}, bf16[256,128]{1,0:T(8,128)(2,1)S(1)}, f32[264,128]{1,0:T(8,128)S(1)}, f32[264,128]{1,0:T(8,128)S(1)}, bf16[2,16,128,256]{3,2,1,0:T(8,128)(2,1)S(1)}) custom-call(bf16[32,1024]{1,0:T(8,128)(2,1)S(1)} %copy-done, bf16[32,1024]{1,0:T(8,128)(2,1)S(1)} %copy-done.1, bf16[32,1024]{1,0:T(8,128)(2,1)S(1)} %copy-done.2, ...), custom_call_target="tpu_custom_call" | custom-call | tf_op jit(solution)/shard_map/gather/pallas_call | solution.py:210
  57.6 0.7 copy.23
  58.3 1.5 %fusion.8 = (bf16[4096,128]{1,0:T(8,128)(2,1)}, bf16[4096,128]{1,0:T(8,128)(2,1)}) fusion(bf16[4096,256]{1,0:T(8,128)(2,1)S(1)} %bitcast.40), kind=kLoop, calls=%fused_computation.17 | loop fusion | bytes 4194304 | tf_op jit(solution)/shard_map/slice | solution.py:513
  59.8 1.5 %copy.26 = bf16[4096,128]{0,1:T(8,128)(2,1)S(1)} copy(bf16[4096,128]{1,0:T(8,128)(2,1)} %get-tuple-element.16) | data formatting | bytes 2097152 | tf_op jit(solution)/shard_map/slice | solution.py:513
  61.4 1.5 %copy.24 = bf16[4096,128]{0,1:T(8,128)(2,1)S(1)} copy(bf16[4096,128]{1,0:T(8,128)(2,1)} %get-tuple-element.17) | data formatting | bytes 2097152 | tf_op jit(solution)/shard_map/slice | solution.py:512
  63.0 5.0 %fusion.9 = (f32[2,256]{1,0:T(2,128)S(1)}, f32[2,256,4096]{2,1,0:T(8,128)}) fusion(bf16[256,2,64]{0,2,1:T(8,128)(2,1)S(1)} %bitcast.52, bf16[4096,2,64]{0,2,1:T(8,128)(2,1)S(1)} %bitcast.45), kind=kOutput, calls=%fused_computation.18 | convolution fusion | flops 274731008 | bytes 9504768 | tf_op jit(solution)/shard_map/sub | solution.py:515
  68.0 4.6 %divide_convert_fusion = bf16[2,256,4096]{2,1,0:T(8,128)(2,1)S(1)} fusion(f32[2,256,4096]{2,1,0:T(8,128)} %get-tuple-element.19, f32[2,256]{1,0:T(2,128)S(1)} %get-tuple-element.18), kind=kLoop, calls=%fused_computation.2 | loop fusion | flops 4194304 | bytes 12584960 | tf_op jit(solution)/shard_map/convert_element_type | solution.py:516
  72.6 1.4 %multiply_reduce_fusion.1 = (f32[256,2]{0,1:T(2,128)S(1)}, bf16[2,64,256]{2,1,0:T(8,128)(2,1)S(1)}) fusion(bf16[256,128]{0,1:T(8,128)(2,1)S(1)} %copy.25, bf16[4096,2,64]{0,2,1:T(8,128)(2,1)S(1)} %bitcast.41, bf16[2,256,4096]{2,1,0:T(8,128)(2,1)S(1)} %divide_convert_fusion), kind=kOutput, calls=%fused_computation.15 | convolution fusion | flops 268598784 | bytes 5376000 | tf_op jit(solution)/shard_map/hqk,khd->qhd/dot_general | solution.py:517
  74.0 0.5 copy-done.8
  74.6 3.2 %convolution_convert_fusion = bf16[2,64,4096]{2,1,0:T(8,128)(2,1)S(1)} fusion(bf16[256,2,64]{0,2,1:T(8,128)(2,1)S(1)} %bitcast.49, bf16[2,256,4096]{2,1,0:T(8,128)(2,1)} %copy-done.8), kind=kOutput, calls=%fused_computation.8 | convolution fusion | flops 268959744 | bytes 5308416 | tf_op jit(solution)/shard_map/hqk,qhd->khd/dot_general | solution.py:523
  77.8 0.2 copy-done.9
  78.1 1.3 multiply_convert_fusion
  79.4 1.4 %fusion.4 = bf16[2,64,256]{2,1,0:T(8,128)(2,1)S(1)} fusion(bf16[4096,2,64]{0,2,1:T(8,128)(2,1)S(1)} %bitcast.46, bf16[2,256,4096]{2,1,0:T(8,128)(2,1)S(1)} %multiply_convert_fusion), kind=kOutput, calls=%fused_computation.12 | convolution fusion | flops 268500992 | bytes 5308416 | tf_op jit(solution)/shard_map/hqk,khd->qhd/dot_general | solution.py:521
  80.9 0.8 fusion.2
  81.7 0.2 copy.31
  82.0 1.7 %copy.27 = bf16[2,16,128,128]{3,2,1,0:T(8,128)(2,1)} copy(bf16[2,16,128,128]{2,1,0,3:T(8,128)(2,1)S(1)} %bitcast.43) | data formatting | bytes 2097152 | tf_op jit(solution)/shard_map/concatenate | solution.py:524
  83.8 0.2 copy.32
  84.1 1.0 copy.28
  85.0 1.5 %pad_maximum_fusion.part = bf16[2,16,128,256]{3,2,1,0:T(8,128)(2,1)S(1)} fusion(bf16[2,16,128,128]{3,2,1,0:T(8,128)(2,1)S(1)} %copy.28, bf16[2,16,128,128]{3,2,1,0:T(8,128)(2,1)} %copy.27), kind=kLoop, calls=%fused_computation.10 | loop fusion | flops 4194304 | bytes 4194304 | tf_op jit(solution)/shard_map/concatenate | solution.py:524
  86.6 47.1 %scatter.1 = (bf16[32,1024]{1,0:T(8,128)(2,1)S(1)}, bf16[32,1024]{1,0:T(8,128)(2,1)S(1)}, bf16[32,1024]{1,0:T(8,128)(2,1)S(1)}, bf16[32,1024]{1,0:T(8,128)(2,1)S...) custom-call(bf16[2,16,128,256]{3,2,1,0:T(8,128)(2,1)S(1)} %pad_maximum_fusion.part, bf16[256,128]{1,0:T(8,128)(2,1)S(1)} %copy.29.att_in, ...), custom_call_target="tpu_custom_call" | custom-call | tf_op jit(solution)/shard_map/scatter/pallas_call | solution.py:469
  133.6 0.6 copy.39
  134.3 0.6 copy.40
  134.9 0.6 copy.41
  135.5 0.6 copy.42
  136.1 0.6 copy.43
  136.7 0.6 copy.44
  (19 shorter events, 0.4 us)
Async XLA Ops:
  0.6 0.8 copy-start
  1.5 0.8 copy-start.1
  2.3 0.8 copy-start.2
  3.2 0.8 copy-start.3
  4.0 0.7 copy-start.4
  4.7 0.7 copy-start.6
  59.8 3.1 %copy-start.10 = (bf16[256,128]{0,1:T(8,128)(2,1)S(1)}, bf16[256,128]{0,1:T(8,128)(2,1)}, u32[]{:S(2)}) copy-start(bf16[256,128]{0,1:T(8,128)(2,1)} %copy.23) | copy-start | bytes 196612
  72.6 1.9 %copy-start.8 = (bf16[2,256,4096]{2,1,0:T(8,128)(2,1)}, bf16[2,256,4096]{2,1,0:T(8,128)(2,1)S(1)}, u32[]{:S(2)}) copy-start(bf16[2,256,4096]{2,1,0:T(8,128)(2,1)S(1)} %divide_convert_fusion) | copy-start | bytes 12582916
  74.6 3.5 %copy-start.9 = (bf16[2,256,4096]{2,1,0:T(8,128)(2,1)S(1)}, bf16[2,256,4096]{2,1,0:T(8,128)(2,1)}, u32[]{:S(2)}) copy-start(bf16[2,256,4096]{2,1,0:T(8,128)(2,1)} %copy-done.8) | copy-start | bytes 12582916
  79.4 1.4 %copy-start.11 = (bf16[256,128]{0,1:T(8,128)(2,1)S(1)}, bf16[256,128]{0,1:T(8,128)(2,1)}, u32[]{:S(2)}) copy-start(bf16[256,128]{0,1:T(8,128)(2,1)} %copy.23) | copy-start | bytes 196612
  83.8 2.8 %copy-start.5 = (f32[3,128]{1,0:T(4,128)S(1)}, f32[3,128]{1,0:T(4,128)}, u32[]{:S(2)}) copy-start(f32[3,128]{1,0:T(4,128)} %kt.3) | copy-start | bytes 4612
  83.8 2.8 %copy-start.7 = (f32[3,128]{1,0:T(4,128)S(1)}, f32[3,128]{1,0:T(4,128)}, u32[]{:S(2)}) copy-start(f32[3,128]{1,0:T(4,128)} %vt.3) | copy-start | bytes 4612

commit v3 on v2

--- a/solution.py
+++ b/solution.py
@@ -7,8 +7,6 @@
 from jax.experimental.pallas import tpu as pltpu
 from jax.sharding import PartitionSpec as P
 
-D = 1024
-HEADS = 16
 MESH = pl.DeviceIdType.MESH
 F32 = jnp.float32
 BF16 = jnp.bfloat16
@@ -501,29 +499,98 @@
     )(part, att, gq, kf, vf, kt, vt)
 
 
+def attention_kernel(block, q_ref, cot_ref, kv_ref, att_ref, gq_ref, part_ref,
+                     s_ref, e_ref, att_t, gq_t):
+    length, ch = q_ref.shape
+    half = ch // 2
+    keys = kv_ref.shape[0]
+    steps = keys // block
+    scaling = half ** (-0.5)
+    lanes = lax.broadcasted_iota(jnp.int32, (length, ch), 1)
+
+    def split(x):
+        x = x.astype(F32)
+        zero = jnp.zeros_like(x)
+        return jnp.concatenate(
+            [jnp.where(lanes < half, x, zero), jnp.where(lanes < half, zero, x)], axis=0).astype(BF16)
+
+    def dot(a, b, ca, cb):
+        return lax.dot_general(a, b, (((ca,), (cb,)), ((), ())), preferred_element_type=F32)
+
+    qs = split(q_ref[...].astype(F32) * scaling)
+    cots = split(cot_ref[...])
+
+    def at(i):
+        return pl.ds(pl.multiple_of(i * block, block), block)
+
+    def scores(i, top):
+        s = dot(kv_ref[at(i), 0:ch], qs, 1, 1)
+        s_ref[at(i), :] = s
+        return jnp.maximum(top, jnp.max(s.reshape(block // 8, 8, 2 * length), axis=0))
+
+    top = lax.fori_loop(0, steps, scores, jnp.full((8, 2 * length), -jnp.inf, F32))
+    top = jnp.max(top, axis=0, keepdims=True)
+
+    att_t[...] = jnp.zeros_like(att_t)
+    gq_t[...] = jnp.zeros_like(gq_t)
+
+    def raise_(i, total):
+        e = jnp.exp(s_ref[at(i), :] - top)
+        eb = e.astype(BF16)
+        e_ref[at(i), :] = eb
+        att_t[...] += dot(kv_ref[at(i), ch:2 * ch], eb, 0, 0)
+        return total + jnp.sum(e.reshape(block // 8, 8, 2 * length), axis=0)
+
+    total = lax.fori_loop(0, steps, raise_, jnp.zeros((8, 2 * length), F32))
+    inv = 1.0 / jnp.sum(total, axis=0, keepdims=True)
+
+    def join(x):
+        return jnp.concatenate([x[0:half, 0:length], x[half:ch, length:2 * length]], axis=0)
+
+    att = jnp.transpose(join(att_t[...] * inv)).astype(BF16)
+    att_ref[...] = att
+    prod = jnp.transpose(cot_ref[...].astype(F32) * att.astype(F32))
+    offset = jnp.concatenate(
+        [jnp.sum(prod[0:half], axis=0, keepdims=True),
+         jnp.sum(prod[half:ch], axis=0, keepdims=True)], axis=1)
+
+    def back(i, carry):
+        w = e_ref[at(i), :].astype(F32) * inv
+        dw = dot(kv_ref[at(i), ch:2 * ch], cots, 1, 1)
+        ds = (w * (dw - offset)).astype(BF16)
+        part_ref[at(i), 0:ch] = dot(ds, qs, 1, 0).astype(BF16)
+        part_ref[at(i), ch:2 * ch] = dot(w.astype(BF16), cots, 1, 0).astype(BF16)
+        gq_t[...] += dot(kv_ref[at(i), 0:ch], ds, 0, 0)
+        return carry
+
+    lax.fori_loop(0, steps, back, 0)
+    gq_ref[...] = (jnp.transpose(join(gq_t[...])) * scaling).astype(BF16)
+
+
 def attention(q, cot, kv):
-    length, channels = q.shape
-    head_dim = D // HEADS
-    heads = channels // head_dim
-    scaling = head_dim ** (-0.5)
-    flat = kv.reshape(-1, 2 * channels)
-    qh = q.reshape(length, heads, head_dim)
-    ch = cot.reshape(length, heads, head_dim)
-    kh = flat[:, :channels].reshape(-1, heads, head_dim)
-    vh = flat[:, channels:].reshape(-1, heads, head_dim)
-    scores = jnp.einsum("qhd,khd->hqk", qh, kh, preferred_element_type=F32) * scaling
-    raised = jnp.exp(scores - jnp.max(scores, axis=2, keepdims=True))
-    weights = (raised / jnp.sum(raised, axis=2, keepdims=True)).astype(BF16)
-    att = jnp.einsum("hqk,khd->qhd", weights, vh, preferred_element_type=F32).astype(BF16)
-    offset = jnp.sum(ch.astype(F32) * att.astype(F32), axis=2)
-    dweights = jnp.einsum("qhd,khd->hqk", ch, vh, preferred_element_type=F32)
-    dscores = (weights.astype(F32) * (dweights - offset.T[:, :, None])).astype(BF16)
-    gq = (jnp.einsum("hqk,khd->qhd", dscores, kh, preferred_element_type=F32) * scaling).astype(BF16)
-    gk = jnp.einsum("hqk,qhd->khd", dscores, qh, preferred_element_type=F32) * scaling
-    gv = jnp.einsum("hqk,qhd->khd", weights, ch, preferred_element_type=F32)
-    part = jnp.concatenate(
-        [gk.reshape(-1, channels), gv.reshape(-1, channels)], axis=1).astype(BF16)
-    return att.reshape(length, channels), gq.reshape(length, channels), part.reshape(kv.shape)
+    length, ch = q.shape
+    flat = kv.reshape(-1, 2 * ch)
+    keys = flat.shape[0]
+    vm = pl.BlockSpec(memory_space=pltpu.VMEM)
+    att, gq, part = pl.pallas_call(
+        functools.partial(attention_kernel, 512),
+        out_shape=(
+            jax.ShapeDtypeStruct((length, ch), BF16),
+            jax.ShapeDtypeStruct((length, ch), BF16),
+            jax.ShapeDtypeStruct((keys, 2 * ch), BF16),
+        ),
+        in_specs=[vm] * 3,
+        out_specs=(vm,) * 3,
+        scratch_shapes=[
+            pltpu.VMEM((keys, 2 * length), F32),
+            pltpu.VMEM((keys, 2 * length), BF16),
+            pltpu.VMEM((ch, 2 * length), F32),
+            pltpu.VMEM((ch, 2 * length), F32),
+        ],
+        compiler_params=pltpu.CompilerParams(vmem_limit_bytes=48 << 20),
+        name="attention",
+    )(q, cot, flat)
+    return att, gq, part.reshape(kv.shape)
 
 
 def local(query_rows, key_rows, value_rows, cotangent, key_taps, value_taps):

time: 138 us -> 120 us (0.87)
  matrix products: 13.2 us -> 0 us
  Pallas kernels: 99.3 us -> 110 us
  local copies, waits for them, and re-layouts: 17.9 us -> 8.39 us
  other arithmetic: 6.1 us -> 0 us
    pallas_call x0 -> x1, Pallas kernels: none -> 10.9 us  [attention(): pl.pallas_call(functools.partial(attention_kernel, 512), out_shape=(jax.S...]
    dot_general x5 -> x0, matrix products: 8.18 us -> none  [the longest x1 3.19 us: attention(): gv = jnp.einsum('hqk,qhd->khd', weights, ch, preferred_element_type=F32)]
    sub x1 -> x0, matrix products: 5 us -> none  [attention(): raised = jnp.exp(scores - jnp.max(scores, axis=2, keepdims=True))]
    convert_element_type x1 -> x0, other arithmetic: 4.62 us -> none  [attention(): weights = (raised / jnp.sum(raised, axis=2, keepdims=True)).astype(BF16)]
    slice x3 -> x0, local copies, waits for them, and re-layouts: 4.48 us -> none  [the longest x2 2.99 us: attention(): vh = flat[:, channels:].reshape(-1, heads, head_dim)]
    concatenate x2 -> x0, local copies, waits for them, and re-layouts: 2.69 us -> none  [attention(): jnp.concatenate([gk.reshape(-1, channels), gv.reshape(-1, channels)], axi...]
    concatenate x1 -> x0, other arithmetic: 1.47 us -> none  [attention(): jnp.concatenate([gk.reshape(-1, channels), gv.reshape(-1, channels)], axi...]
    unnamed x32 -> x22, local copies, waits for them, and re-layouts: 9.66 us -> 8.39 us
where the time goes in v3:
time: 120 us
  Pallas kernels  110 us (92%)
  local copies, waits for them, and re-layouts  8.39 us (7%)
    pallas_call x1, Pallas kernels, gather(): pl.pallas_call(functools.partial(gather_kernel, nz, nh), out_shape=(jax.S...  52.4 us
    pallas_call x1, Pallas kernels, scatter(): pl.pallas_call(functools.partial(scatter_kernel, nz, nh), out_shape=(wide...  47.2 us
    pallas_call x1, Pallas kernels, attention(): pl.pallas_call(functools.partial(attention_kernel, 512), out_shape=(jax.S...  10.9 us
    unnamed x22, local copies, waits for them, and re-layouts  8.39 us

profile of v3, /device:TPU:1, one launch (start us, length us, event | category | flops | bytes accessed | tf_op | source)
XLA Modules:
  0.0 119.5 jit_solution(17467193219797127783)
XLA Ops:
  0.6 0.0 copy-start
  0.6 0.8 copy-done
  1.5 0.0 copy-start.1
  1.5 0.8 copy-done.1
  2.3 0.0 copy-start.2
  2.3 0.8 copy-done.2
  3.2 0.0 copy-start.3
  3.2 0.8 copy-done.3
  4.0 0.0 copy-start.4
  4.0 0.7 copy-done.4
  4.7 0.0 copy-start.6
  4.7 0.7 copy-done.6
  5.4 0.0 copy-start.5
  5.4 0.0 copy-start.7
  5.4 52.4 %gather.1 = (bf16[256,128]{1,0:T(8,128)(2,1)S(1)}, bf16[256,128]{1,0:T(8,128)(2,1)S(1)}, f32[264,128]{1,0:T(8,128)S(1)}, f32[264,128]{1,0:T(8,128)S(1)}, bf16[2,16,128,256]{3,2,1,0:T(8,128)(2,1)S(1)}) custom-call(bf16[32,1024]{1,0:T(8,128)(2,1)S(1)} %copy-done, bf16[32,1024]{1,0:T(8,128)(2,1)S(1)} %copy-done.1, bf16[32,1024]{1,0:T(8,128)(2,1)S(1)} %copy-done.2, ...), custom_call_target="tpu_custom_call" | custom-call | tf_op jit(solution)/shard_map/gather/pallas_call | solution.py:208
  57.7 10.9 %attention.1 = (bf16[256,128]{1,0:T(8,128)(2,1)S(1)}, bf16[256,128]{1,0:T(8,128)(2,1)S(1)}, bf16[4096,256]{1,0:T(8,128)(2,1)S(1)}) custom-call(bf16[256,128]{1,0:T(8,128)(2,1)S(1)} %get-tuple-element.14.q_ref, bf16[256,128]{1,0:T(8,128)(2,1)S(1)} %get-tuple-element.15.cot_ref, bf16[4096,256]{1,0:T(8,128)(2,1)S(1)} %bitcast.3), custom_call_target="tpu_custom_call" | custom-call | tf_op jit(solution)/shard_map/attention/pallas_call | solution.py:575
  68.6 0.0 copy-done.5
  68.7 0.0 copy-done.7
  68.7 47.2 %scatter.1 = (bf16[32,1024]{1,0:T(8,128)(2,1)S(1)}, bf16[32,1024]{1,0:T(8,128)(2,1)S(1)}, bf16[32,1024]{1,0:T(8,128)(2,1)S(1)}, bf16[32,1024]{1,0:T(8,128)(2,1)S...) custom-call(bf16[2,16,128,256]{3,2,1,0:T(8,128)(2,1)S(1)} %bitcast.2, bf16[256,128]{1,0:T(8,128)(2,1)S(1)} %get-tuple-element.18.att_in, ...), custom_call_target="tpu_custom_call" | custom-call | tf_op jit(solution)/shard_map/scatter/pallas_call | solution.py:467
  115.8 0.6 copy.18
  116.5 0.6 copy.19
  117.1 0.6 copy.20
  117.7 0.6 copy.21
  118.3 0.6 copy.22
  118.9 0.6 copy.23
Async XLA Ops:
  0.6 0.8 copy-start
  1.5 0.8 copy-start.1
  2.3 0.8 copy-start.2
  3.2 0.8 copy-start.3
  4.0 0.7 copy-start.4
  4.7 0.7 copy-start.6
  5.4 63.3 %copy-start.5 = (f32[3,128]{1,0:T(4,128)S(1)}, f32[3,128]{1,0:T(4,128)}, u32[]{:S(2)}) copy-start(f32[3,128]{1,0:T(4,128)} %kt.3) | copy-start | bytes 4612
  5.4 63.3 %copy-start.7 = (f32[3,128]{1,0:T(4,128)S(1)}, f32[3,128]{1,0:T(4,128)}, u32[]{:S(2)}) copy-start(f32[3,128]{1,0:T(4,128)} %vt.3) | copy-start | bytes 4612

commit v4 on v3

--- a/solution.py
+++ b/solution.py
@@ -9,6 +9,7 @@
 
 MESH = pl.DeviceIdType.MESH
 F32 = jnp.float32
+JUMP = 5
 BF16 = jnp.bfloat16
 
 
@@ -44,7 +45,7 @@
                   q_out, cot_out, kf, vf, kv,
                   k_loc, v_loc, halo,
                   a_send, a_recv, a_self, h_send, h_recv,
-                  y_send, y_recv, r_send, r_recv, l_send, l_recv, c_send, c_recv):
+                  y_send, y_recv, r_send, r_recv, l_send, l_recv, c_send, c_recv, j_send, j_recv):
     ctx, head, y, z, core = place(nz)
     nctx = 4 * nz
     rows = q_in.shape[0]
@@ -62,6 +63,9 @@
         greet(barrier, ctx, (head + p) % nh)
     for other in (right, left, across, mate):
         greet(barrier, other, head)
+    for side in range(2):
+        for step in (JUMP, nz - JUMP):
+            greet(barrier, ctx_of(nz, side, (z + step) % nz, core), head)
 
     @pl.when(takes)
     def _():
@@ -69,11 +73,11 @@
 
     @pl.when(gives)
     def _():
-        pl.semaphore_wait(barrier, nh - 1 + 4 + nh)
+        pl.semaphore_wait(barrier, nh - 1 + 8 + nh)
 
     @pl.when(jnp.logical_not(gives))
     def _():
-        pl.semaphore_wait(barrier, nh - 1 + 4)
+        pl.semaphore_wait(barrier, nh - 1 + 8)
 
     pairs = ((k_in, k_loc), (v_in, v_loc), (q_in, q_out), (cot_in, cot_out))
 
@@ -139,54 +143,100 @@
     def to_mate(zz, u, n):
         return remote(chunk(zz, u), chunk(zz, u), c_send.at[n, u], c_recv.at[n, u], mate, head)
 
-    def to_right(s, u):
-        here = chunk((z + nz - s) % nz, u)
-        return remote(here, here, r_send.at[s, u], r_recv.at[s, u], right, head)
-
-    def to_left(s, u):
-        here = chunk((z + s) % nz, u)
-        return remote(here, here, l_send.at[s, u], l_recv.at[s, u], left, head)
-
-    nr, nl = nz // 2, nz // 2 - 1
+    flows = ((0, 2, 2), (-JUMP, nz // 2 - JUMP, nz // 2 - 1 - JUMP), (JUMP, 2, 2))
+
+    def to_right(f, k, u):
+        here = chunk((z + flows[f][0] - k + 2 * nz) % nz, u)
+        return remote(here, here, r_send.at[3 * f + k, u], r_recv.at[3 * f + k, u], right, head)
+
+    def to_left(f, k, u):
+        here = chunk((z + left_of[f] + k + 2 * nz) % nz, u)
+        return remote(here, here, l_send.at[3 * f + k, u], l_recv.at[3 * f + k, u], left, head)
+
+    left_of = (0, JUMP, -JUMP)
+
+    def jump(sign, u):
+        side = y + u - 2 * u * y
+        here = chunk(z, 0)
+        return remote(here, here, j_send.at[sign, u], j_recv.at[sign, u],
+                      ctx_of(nz, side, (z + (2 * sign - 1) * JUMP + nz) % nz, core), head)
+
     step_y = remote(chunk(z, 0), chunk(z, 0), y_send, y_recv, across, head)
+    mates = []
+
+    def forward(zz, u, n):
+        mates.append(to_mate(zz, u, n))
+        mates[-1].start()
+
+    begun = []
+
+    def go(copy):
+        copy.start()
+        begun.append(copy)
+
+    for sign in range(2):
+        go(jump(sign, 0))
+    go(to_right(0, 0, 0))
+    go(to_left(0, 0, 0))
     step_y.start()
-    to_right(0, 0).start()
-    to_left(0, 0).start()
-    mates = [to_mate(z, 0, 0)]
-    mates[0].start()
+    for sign in range(2):
+        go(jump(sign, 1))
+    forward(z, 0, 0)
     for a in range(2, 4):
         own(a).start()
         for m in moves[a]:
             m.start()
+
+    def got_right(f, k, u):
+        to_right(f, k, u).wait_recv()
+        if k + 1 < flows[f][1]:
+            go(to_right(f, k + 1, u))
+        forward((z - 1 + flows[f][0] - k + 2 * nz) % nz, u, 1 + 3 * f + k)
+
+    def got_left(f, k, u):
+        to_left(f, k, u).wait_recv()
+        if k + 1 < flows[f][2]:
+            go(to_left(f, k + 1, u))
+        forward((z + 1 + left_of[f] + k + 2 * nz) % nz, u, 10 + 3 * f + k)
+
+    got_right(0, 0, 0)
+    got_left(0, 0, 0)
     step_y.wait_recv()
-    to_right(0, 1).start()
-    to_left(0, 1).start()
-    mates.append(to_mate(z, 1, 0))
-    mates[1].start()
-    for s in range(nr):
+    go(to_right(0, 0, 1))
+    go(to_left(0, 0, 1))
+    forward(z, 1, 0)
+    for u in range(2):
+        for sign in (1, 0):
+            jump(sign, u).wait_recv()
+            if sign == 1:
+                go(to_right(1, 0, u))
+                go(to_left(2, 0, u))
+            else:
+                go(to_right(2, 0, u))
+                go(to_left(1, 0, u))
+            forward((z - (2 * sign - 1) * JUMP + nz) % nz, u, 19 + sign)
+    got_right(0, 1, 0)
+    got_left(0, 1, 0)
+    got_right(0, 0, 1)
+    got_left(0, 0, 1)
+    for k in range(3):
         for u in range(2):
-            to_right(s, u).wait_recv()
-            if s + 1 < nr:
-                to_right(s + 1, u).start()
-            mates.append(to_mate((z + nz - s - 1) % nz, u, 1 + s))
-            mates[-1].start()
-            if s < nl:
-                to_left(s, u).wait_recv()
-                if s + 1 < nl:
-                    to_left(s + 1, u).start()
-                mates.append(to_mate((z + s + 1) % nz, u, 1 + nr + s))
-                mates[-1].start()
+            for f in (1, 2):
+                if k < flows[f][1]:
+                    got_right(f, k, u)
+                if k < flows[f][2]:
+                    got_left(f, k, u)
+        if k == 0:
+            got_right(0, 1, 1)
+            got_left(0, 1, 1)
     for a in range(2, 4):
         own(a).wait()
         for m in moves[a]:
             m.wait_recv()
     for m in mates:
         m.wait()
-    for u in range(2):
-        for s in range(nr):
-            to_right(s, u).wait_send()
-        for s in range(nl):
-            to_left(s, u).wait_send()
+    for m in begun:
+        m.wait_send()
     step_y.wait_send()
     for a in range(4):
         for m in moves[a]:
@@ -223,9 +273,10 @@
             dma((4, nh - 1)), dma((4, nh - 1)), dma((4,)),
             dma((2, nh)), dma((2,)),
             dma(()), dma(()),
-            dma((nz // 2, 2)), dma((nz // 2, 2)),
-            dma((nz // 2 - 1, 2)), dma((nz // 2 - 1, 2)),
-            dma((nz, 2)), dma((nz, 2)),
+            dma((9, 2)), dma((9, 2)),
+            dma((9, 2)), dma((9, 2)),
+            dma((21, 2)), dma((21, 2)),
+            dma((2, 2)), dma((2, 2)),
         ],
         compiler_params=pltpu.CompilerParams(
             collective_id=0, has_side_effects=True, vmem_limit_bytes=40 << 20),
@@ -235,11 +286,11 @@
 
 def scatter_kernel(nz, nh, part, att_in, gq_in, kf, vf, kt, vt,
                    att_out, gq_out, gk_out, gv_out, kt_out, vt_out,
-                   pin, rbuf, rout, lbuf, lout, ybuf, yout, spread, gk_loc, gv_loc,
+                   pin, rbuf, rout, lbuf, lout, jbuf, jout, ybuf, yout, spread, gk_loc, gv_loc,
                    edge, edge_in, tap1, tap2,
                    a_send, a_recv, a_self, e_send, e_recv,
                    y_send, y_recv, r_send, r_recv, l_send, l_recv, c_send, c_recv,
-                   t_send, t_recv, u_send, u_recv):
+                   t_send, t_recv, u_send, u_recv, j_send, j_recv):
     ctx, head, y, z, core = place(nz)
     nctx = 4 * nz
     rows = att_out.shape[0]
@@ -275,17 +326,12 @@
     def _():
         pl.semaphore_wait(barrier, nh - 1 + nz - 1 + 3)
 
-    nr, nl = nz // 2, nz // 2 - 1
 
     def to_mate(zz, n):
         return remote(part.at[1 - core, zz], pin.at[zz], c_send.at[n], c_recv.at[n], mate, head)
 
-    order = []
-    for s in range(nr):
-        order.append((z + nz // 2 + nz - s) % nz)
-        if s < nl:
-            order.append((z + nz - nl + s) % nz)
-    order.append(z)
+    offsets = (-8, 7, 3, -3, -7, 6, 4, -4, -6, -5, 5, -2, 2, -1, 1, 0)
+    order = [(z + o + 2 * nz) % nz for o in offsets]
     mates = [to_mate(zz, n) for n, zz in enumerate(order)]
     for m in mates:
         m.start()
@@ -315,40 +361,81 @@
         side = 1 - y - u + 2 * u * y
         return pl.ds(pl.multiple_of(side * count, count), count)
 
-    def local_sum(n, u):
+    def local_sum(o, u):
+        n = offsets.index(o)
         if u == 0:
             mates[n].wait_recv()
         zz = order[n]
         return part[core, zz, part_of(u), :].astype(F32) + pin[zz, part_of(u), :].astype(F32)
 
-    def to_right(s, u):
-        return remote(rout.at[s, u], rbuf.at[s, u], r_send.at[s, u], r_recv.at[s, u], right, head)
-
-    def to_left(s, u):
-        return remote(lout.at[s, u], lbuf.at[s, u], l_send.at[s, u], l_recv.at[s, u], left, head)
-
-    for s in range(nr):
+    lefts = ((-8, -7, -6), (3, 4), (-2, -1))
+    rights = ((7, 6), (-3, -4), (2, 1))
+
+    def to_right(f, k, u):
+        return remote(rout.at[3 * f + k, u], rbuf.at[3 * f + k, u],
+                      r_send.at[3 * f + k, u], r_recv.at[3 * f + k, u], right, head)
+
+    def to_left(f, k, u):
+        return remote(lout.at[3 * f + k, u], lbuf.at[3 * f + k, u],
+                      l_send.at[3 * f + k, u], l_recv.at[3 * f + k, u], left, head)
+
+    def jump(sign, u):
+        return remote(jout.at[sign, u], jbuf.at[sign, u], j_send.at[sign, u], j_recv.at[sign, u],
+                      ctx_of(nz, y, (z + (2 * sign - 1) * JUMP + nz) % nz, core), head)
+
+    begun = []
+
+    def from_left(f, k, u):
+        to_right(f, k, u).wait_recv()
+        return rbuf[3 * f + k, u].astype(F32)
+
+    def from_right(f, k, u):
+        to_left(f, k, u).wait_recv()
+        return lbuf[3 * f + k, u].astype(F32)
+
+    def push_right(f, k, u):
+        total = local_sum(rights[f][k], u)
+        if k > 0:
+            total = total + from_left(f, k - 1, u)
+        rout[3 * f + k, u] = total.astype(BF16)
+        begun.append(to_right(f, k, u))
+        begun[-1].start()
+
+    def push_left(f, k, u):
+        total = local_sum(lefts[f][k], u)
+        if k > 0:
+            total = total + from_right(f, k - 1, u)
+        lout[3 * f + k, u] = total.astype(BF16)
+        begun.append(to_left(f, k, u))
+        begun[-1].start()
+
+    def push_jump(sign, total, u):
+        jout[sign, u] = total.astype(BF16)
+        begun.append(jump(sign, u))
+        begun[-1].start()
+
+    for k in range(2):
         for u in range(2):
-            n = 2 * s
-            total = local_sum(n, u)
-            if s > 0:
-                to_right(s - 1, u).wait_recv()
-                total = total + rbuf[s - 1, u].astype(F32)
-            rout[s, u] = total.astype(BF16)
-            to_right(s, u).start()
-            if s < nl:
-                total = local_sum(n + 1, u)
-                if s > 0:
-                    to_left(s - 1, u).wait_recv()
-                    total = total + lbuf[s - 1, u].astype(F32)
-                lout[s, u] = total.astype(BF16)
-                to_left(s, u).start()
+            push_left(0, k, u)
+            push_right(0, k, u)
+            push_left(1, k, u)
+            push_right(1, k, u)
     for u in range(2):
-        total = local_sum(2 * nr - 1, u)
-        to_left(nl - 1, u).wait_recv()
-        total = total + lbuf[nl - 1, u].astype(F32)
-        to_right(nr - 1, u).wait_recv()
-        total = total + rbuf[nr - 1, u].astype(F32)
+        push_left(0, 2, u)
+    for u in range(2):
+        push_left(2, 0, u)
+        push_right(2, 0, u)
+    for u in range(2):
+        push_jump(1, local_sum(5, u) + from_left(0, 1, u) + from_right(1, 1, u), u)
+    for u in range(2):
+        push_left(2, 1, u)
+        push_right(2, 1, u)
+        push_jump(0, local_sum(-5, u) + from_right(0, 2, u) + from_left(1, 1, u), u)
+    for u in range(2):
+        total = local_sum(0, u) + from_right(2, 1, u) + from_left(2, 1, u)
+        for sign in range(2):
+            jump(sign, u).wait_recv()
+            total = total + jbuf[sign, u].astype(F32)
         if u == 0:
             ybuf[...] = total.astype(BF16)
             step_y = remote(ybuf, yout, y_send, y_recv, across, head)
@@ -435,11 +522,8 @@
 
     for m in mates:
         m.wait_send()
-    for u in range(2):
-        for s in range(nr):
-            to_right(s, u).wait_send()
-        for s in range(nl):
-            to_left(s, u).wait_send()
+    for m in begun:
+        m.wait_send()
     step_y.wait_send()
     for a in range(4):
         for m in moves[a]:
@@ -461,7 +545,6 @@
     count = length // 4
     vm = pl.BlockSpec(memory_space=pltpu.VMEM)
     dma = pltpu.SemaphoreType.DMA
-    nr, nl = nz // 2, nz // 2 - 1
     wide = jax.ShapeDtypeStruct((rows, nh * ch), BF16)
     small = jax.ShapeDtypeStruct((3, ch), F32)
     return pl.pallas_call(
@@ -471,10 +554,12 @@
         out_specs=(vm,) * 6,
         scratch_shapes=[
             pltpu.VMEM((nz, 2 * count, 2 * ch), BF16),
-            pltpu.VMEM((nr, 2, count, 2 * ch), BF16),
-            pltpu.VMEM((nr, 2, count, 2 * ch), BF16),
-            pltpu.VMEM((nl, 2, count, 2 * ch), BF16),
-            pltpu.VMEM((nl, 2, count, 2 * ch), BF16),
+            pltpu.VMEM((9, 2, count, 2 * ch), BF16),
+            pltpu.VMEM((9, 2, count, 2 * ch), BF16),
+            pltpu.VMEM((9, 2, count, 2 * ch), BF16),
+            pltpu.VMEM((9, 2, count, 2 * ch), BF16),
+            pltpu.VMEM((2, 2, count, 2 * ch), BF16),
+            pltpu.VMEM((2, 2, count, 2 * ch), BF16),
             pltpu.VMEM((count, 2 * ch), BF16),
             pltpu.VMEM((count, 2 * ch), BF16),
             pltpu.VMEM((2, length + 16, ch), F32),
@@ -487,11 +572,12 @@
             dma((4, nh - 1)), dma((4, nh - 1)), dma((4,)),
             dma((2,)), dma((2, nh)),
             dma(()), dma(()),
-            dma((nr, 2)), dma((nr, 2)),
-            dma((nl, 2)), dma((nl, 2)),
+            dma((9, 2)), dma((9, 2)),
+            dma((9, 2)), dma((9, 2)),
             dma((nz,)), dma((nz,)),
             dma((nz - 1,)), dma((nz - 1,)),
             dma((3,)), dma((3,)),
+            dma((2, 2)), dma((2, 2)),
         ],
         compiler_params=pltpu.CompilerParams(
             collective_id=1, has_side_effects=True, vmem_limit_bytes=40 << 20),

time: 120 us -> 113 us (0.942)
  Pallas kernels: 110 us -> 103 us
    pallas_call x1, Pallas kernels: 52.4 us -> 47.7 us  [gather(): pl.pallas_call(functools.partial(gather_kernel, nz, nh), out_shape=(jax.S...]
    pallas_call x1, Pallas kernels: 47.2 us -> 44.8 us  [scatter(): pl.pallas_call(functools.partial(scatter_kernel, nz, nh), out_shape=(wide...]
where the time goes in v4:
time: 113 us
  Pallas kernels  103 us (91%)
  local copies, waits for them, and re-layouts  8.39 us (7%)
    pallas_call x1, Pallas kernels, gather(): pl.pallas_call(functools.partial(gather_kernel, nz, nh), out_shape=(jax.S...  47.7 us
    pallas_call x1, Pallas kernels, scatter(): pl.pallas_call(functools.partial(scatter_kernel, nz, nh), out_shape=(wide...  44.8 us
    pallas_call x1, Pallas kernels, attention(): pl.pallas_call(functools.partial(attention_kernel, 512), out_shape=(jax.S...  10.9 us
    unnamed x22, local copies, waits for them, and re-layouts  8.39 us

profile of v4, /device:TPU:1, one launch (start us, length us, event | category | flops | bytes accessed | tf_op | source)
XLA Modules:
  0.0 112.5 jit_solution(15851133861810062970)
XLA Ops:
  0.6 0.0 copy-start
  0.6 0.8 copy-done
  1.5 0.0 copy-start.1
  1.5 0.8 copy-done.1
  2.3 0.0 copy-start.2
  2.3 0.8 copy-done.2
  3.2 0.0 copy-start.3
  3.2 0.8 copy-done.3
  4.0 0.0 copy-start.4
  4.0 0.7 copy-done.4
  4.7 0.0 copy-start.6
  4.7 0.7 copy-done.6
  5.4 0.0 copy-start.5
  5.4 0.0 copy-start.7
  5.4 47.7 %gather.1 = (bf16[256,128]{1,0:T(8,128)(2,1)S(1)}, bf16[256,128]{1,0:T(8,128)(2,1)S(1)}, f32[264,128]{1,0:T(8,128)S(1)}, f32[264,128]{1,0:T(8,128)S(1)}, bf16[2,16,128,256]{3,2,1,0:T(8,128)(2,1)S(1)}) custom-call(bf16[32,1024]{1,0:T(8,128)(2,1)S(1)} %copy-done, bf16[32,1024]{1,0:T(8,128)(2,1)S(1)} %copy-done.1, bf16[32,1024]{1,0:T(8,128)(2,1)S(1)} %copy-done.2, ...), custom_call_target="tpu_custom_call" | custom-call | tf_op jit(solution)/shard_map/gather/pallas_call | solution.py:258
  53.1 10.9 %attention.1 = (bf16[256,128]{1,0:T(8,128)(2,1)S(1)}, bf16[256,128]{1,0:T(8,128)(2,1)S(1)}, bf16[4096,256]{1,0:T(8,128)(2,1)S(1)}) custom-call(bf16[256,128]{1,0:T(8,128)(2,1)S(1)} %get-tuple-element.14.q_ref, bf16[256,128]{1,0:T(8,128)(2,1)S(1)} %get-tuple-element.15.cot_ref, bf16[4096,256]{1,0:T(8,128)(2,1)S(1)} %bitcast.3), custom_call_target="tpu_custom_call" | custom-call | tf_op jit(solution)/shard_map/attention/pallas_call | solution.py:661
  64.0 0.0 copy-done.5
  64.0 0.0 copy-done.7
  64.0 44.8 %scatter.1 = (bf16[32,1024]{1,0:T(8,128)(2,1)S(1)}, bf16[32,1024]{1,0:T(8,128)(2,1)S(1)}, bf16[32,1024]{1,0:T(8,128)(2,1)S(1)}, bf16[32,1024]{1,0:T(8,128)(2,1)S...) custom-call(bf16[2,16,128,256]{3,2,1,0:T(8,128)(2,1)S(1)} %bitcast.2, bf16[256,128]{1,0:T(8,128)(2,1)S(1)} %get-tuple-element.18.att_in, ...), custom_call_target="tpu_custom_call" | custom-call | tf_op jit(solution)/shard_map/scatter/pallas_call | solution.py:550
  108.8 0.6 copy.18
  109.5 0.6 copy.19
  110.1 0.6 copy.20
  110.7 0.6 copy.21
  111.4 0.6 copy.22
  111.9 0.6 copy.23
Async XLA Ops:
  0.6 0.8 copy-start
  1.5 0.8 copy-start.1
  2.3 0.8 copy-start.2
  3.2 0.8 copy-start.3
  4.0 0.7 copy-start.4
  4.7 0.7 copy-start.6
  5.4 58.7 %copy-start.5 = (f32[3,128]{1,0:T(4,128)S(1)}, f32[3,128]{1,0:T(4,128)}, u32[]{:S(2)}) copy-start(f32[3,128]{1,0:T(4,128)} %kt.3) | copy-start | bytes 4612
  5.4 58.7 %copy-start.7 = (f32[3,128]{1,0:T(4,128)S(1)}, f32[3,128]{1,0:T(4,128)}, u32[]{:S(2)}) copy-start(f32[3,128]{1,0:T(4,128)} %vt.3) | copy-start | bytes 4612

commit v5 on v4

--- a/solution.py
+++ b/solution.py
@@ -114,6 +114,11 @@
         for m in halo_copies():
             m.start()
 
+    for a in range(2, 4):
+        own(a).start()
+        for m in moves[a]:
+            m.start()
+
     @pl.when(jnp.logical_not(takes))
     def _():
         kf[0:8, :] = jnp.zeros((8, ch), F32)
@@ -182,10 +187,6 @@
     for sign in range(2):
         go(jump(sign, 1))
     forward(z, 0, 0)
-    for a in range(2, 4):
-        own(a).start()
-        for m in moves[a]:
-            m.start()
 
     def got_right(f, k, u):
         to_right(f, k, u).wait_recv()
@@ -352,11 +353,6 @@
             pairs[a][0].at[col(head, rows), :], pairs[a][1].at[:, col(head, ch)], a_self.at[a])
 
     moves = [swaps(a) for a in range(4)]
-    for a in range(2):
-        own(a).start()
-        for m in moves[a]:
-            m.start()
-
     def part_of(u):
         side = 1 - y - u + 2 * u * y
         return pl.ds(pl.multiple_of(side * count, count), count)
@@ -420,6 +416,11 @@
             push_right(0, k, u)
             push_left(1, k, u)
             push_right(1, k, u)
+        if k == 0:
+            for a in range(2):
+                own(a).start()
+                for m in moves[a]:
+                    m.start()
     for u in range(2):
         push_left(0, 2, u)
     for u in range(2):
@@ -445,7 +446,23 @@
             grads = total + yout[...].astype(F32)
 
     tap1[z, 6:8, :] = jnp.zeros((2, ch), F32)
-    for a, f, taps, loc in ((0, kf, kt, gk_loc), (1, vf, vt, gv_loc)):
+    for a, f in ((0, kf), (1, vf)):
+        g = grads[:, a * ch:(a + 1) * ch]
+        for t in range(3):
+            tap1[z, 3 * a + t:3 * a + t + 1, :] = jnp.sum(
+                g * f[pl.ds(7 + t, count, stride=4), :], axis=0, keepdims=True)
+
+    def tap_z():
+        out = []
+        for p in range(1, nz):
+            out.append(remote(tap1.at[z], tap1.at[z], t_send.at[p - 1], t_recv.at[p - 1],
+                              ctx_of(nz, y, (z + p) % nz, core), head))
+        return out
+
+    for m in tap_z():
+        m.start()
+
+    for a, taps, loc in ((0, kt, gk_loc), (1, vt, gv_loc)):
         g = grads[:, a * ch:(a + 1) * ch]
         spread[a, 0:8, :] = jnp.zeros((8, ch), F32)
         spread[a, pl.ds(nh * rows, 8), :] = jnp.zeros((8, ch), F32)
@@ -456,16 +473,6 @@
         spread[a, pl.ds(nh * rows + 7, 1), :] = jnp.zeros((1, ch), F32)
         loc[...] = spread[a, pl.ds(8, nh * rows), :].astype(BF16)
         edge[a] = jnp.concatenate([jnp.zeros((8, ch), F32), spread[a, 0:8, :]], axis=0).astype(BF16)
-        for t in range(3):
-            tap1[z, 3 * a + t:3 * a + t + 1, :] = jnp.sum(
-                g * f[pl.ds(7 + t, count, stride=4), :], axis=0, keepdims=True)
-
-    def tap_z():
-        out = []
-        for p in range(1, nz):
-            out.append(remote(tap1.at[z], tap1.at[z], t_send.at[p - 1], t_recv.at[p - 1],
-                              ctx_of(nz, y, (z + p) % nz, core), head))
-        return out
 
     def tap_yc():
         out = []
@@ -477,9 +484,6 @@
     def edges():
         return [remote(edge.at[a], edge_in.at[a, head], e_send.at[a], e_recv.at[a, head],
                        ctx - 1, last) for a in range(2)]
-
-    for m in tap_z():
-        m.start()
 
     @pl.when(gives)
     def _():

time: 113 us -> 113 us (level)
  no operation moved by 1% of the time
where the time goes in v5:
time: 113 us
  Pallas kernels  104 us (92%)
  local copies, waits for them, and re-layouts  8.39 us (7%)
    pallas_call x1, Pallas kernels, gather(): pl.pallas_call(functools.partial(gather_kernel, nz, nh), out_shape=(jax.S...  48.9 us
    pallas_call x1, Pallas kernels, scatter(): pl.pallas_call(functools.partial(scatter_kernel, nz, nh), out_shape=(wide...  44 us
    pallas_call x1, Pallas kernels, attention(): pl.pallas_call(functools.partial(attention_kernel, 512), out_shape=(jax.S...  10.9 us
    unnamed x22, local copies, waits for them, and re-layouts  8.39 us

profile of v5, /device:TPU:1, one launch (start us, length us, event | category | flops | bytes accessed | tf_op | source)
XLA Modules:
  0.0 112.9 jit_solution(3984758202971798585)
XLA Ops:
  0.6 0.0 copy-start
  0.6 0.8 copy-done
  1.5 0.0 copy-start.1
  1.5 0.8 copy-done.1
  2.3 0.0 copy-start.2
  2.3 0.8 copy-done.2
  3.2 0.0 copy-start.3
  3.2 0.8 copy-done.3
  4.0 0.0 copy-start.4
  4.0 0.7 copy-done.4
  4.7 0.0 copy-start.6
  4.7 0.7 copy-done.6
  5.4 0.0 copy-start.5
  5.4 0.0 copy-start.7
  5.4 48.9 %gather.1 = (bf16[256,128]{1,0:T(8,128)(2,1)S(1)}, bf16[256,128]{1,0:T(8,128)(2,1)S(1)}, f32[264,128]{1,0:T(8,128)S(1)}, f32[264,128]{1,0:T(8,128)S(1)}, bf16[2,16,128,256]{3,2,1,0:T(8,128)(2,1)S(1)}) custom-call(bf16[32,1024]{1,0:T(8,128)(2,1)S(1)} %copy-done, bf16[32,1024]{1,0:T(8,128)(2,1)S(1)} %copy-done.1, bf16[32,1024]{1,0:T(8,128)(2,1)S(1)} %copy-done.2, ...), custom_call_target="tpu_custom_call" | custom-call | tf_op jit(solution)/shard_map/gather/pallas_call | solution.py:259
  54.2 10.9 %attention.1 = (bf16[256,128]{1,0:T(8,128)(2,1)S(1)}, bf16[256,128]{1,0:T(8,128)(2,1)S(1)}, bf16[4096,256]{1,0:T(8,128)(2,1)S(1)}) custom-call(bf16[256,128]{1,0:T(8,128)(2,1)S(1)} %get-tuple-element.14.q_ref, bf16[256,128]{1,0:T(8,128)(2,1)S(1)} %get-tuple-element.15.cot_ref, bf16[4096,256]{1,0:T(8,128)(2,1)S(1)} %bitcast.3), custom_call_target="tpu_custom_call" | custom-call | tf_op jit(solution)/shard_map/attention/pallas_call | solution.py:665
  65.2 0.0 copy-done.5
  65.2 0.0 copy-done.7
  65.2 44.0 %scatter.1 = (bf16[32,1024]{1,0:T(8,128)(2,1)S(1)}, bf16[32,1024]{1,0:T(8,128)(2,1)S(1)}, bf16[32,1024]{1,0:T(8,128)(2,1)S(1)}, bf16[32,1024]{1,0:T(8,128)(2,1)S...) custom-call(bf16[2,16,128,256]{3,2,1,0:T(8,128)(2,1)S(1)} %bitcast.2, bf16[256,128]{1,0:T(8,128)(2,1)S(1)} %get-tuple-element.18.att_in, ...), custom_call_target="tpu_custom_call" | custom-call | tf_op jit(solution)/shard_map/scatter/pallas_call | solution.py:554
  109.2 0.6 copy.18
  109.8 0.6 copy.19
  110.4 0.6 copy.20
  111.1 0.6 copy.21
  111.7 0.6 copy.22
  112.3 0.6 copy.23
Async XLA Ops:
  0.6 0.8 copy-start
  1.5 0.8 copy-start.1
  2.3 0.8 copy-start.2
  3.2 0.8 copy-start.3
  4.0 0.7 copy-start.4
  4.7 0.7 copy-start.6
  5.4 59.8 %copy-start.5 = (f32[3,128]{1,0:T(4,128)S(1)}, f32[3,128]{1,0:T(4,128)}, u32[]{:S(2)}) copy-start(f32[3,128]{1,0:T(4,128)} %kt.3) | copy-start | bytes 4612
  5.4 59.8 %copy-start.7 = (f32[3,128]{1,0:T(4,128)S(1)}, f32[3,128]{1,0:T(4,128)}, u32[]{:S(2)}) copy-start(f32[3,128]{1,0:T(4,128)} %vt.3) | copy-start | bytes 4612

commit v6 on v5

--- a/solution.py
+++ b/solution.py
@@ -114,11 +114,6 @@
         for m in halo_copies():
             m.start()
 
-    for a in range(2, 4):
-        own(a).start()
-        for m in moves[a]:
-            m.start()
-
     @pl.when(jnp.logical_not(takes))
     def _():
         kf[0:8, :] = jnp.zeros((8, ch), F32)
@@ -187,6 +182,10 @@
     for sign in range(2):
         go(jump(sign, 1))
     forward(z, 0, 0)
+    for a in range(2, 4):
+        own(a).start()
+        for m in moves[a]:
+            m.start()
 
     def got_right(f, k, u):
         to_right(f, k, u).wait_recv()

time: 113 us -> 113 us (level)
  no operation moved by 1% of the time
where the time goes in v6:
time: 113 us; the launch traced here: 112 us
  Pallas kernels  103 us (91%)
  local copies, waits for them, and re-layouts  8.39 us (7%)
    pallas_call x1, Pallas kernels, gather(): pl.pallas_call(functools.partial(gather_kernel, nz, nh), out_shape=(jax.S...  47.7 us
    pallas_call x1, Pallas kernels, scatter(): pl.pallas_call(functools.partial(scatter_kernel, nz, nh), out_shape=(wide...  44.8 us
    pallas_call x1, Pallas kernels, attention(): pl.pallas_call(functools.partial(attention_kernel, 512), out_shape=(jax.S...  10.9 us
    unnamed x22, local copies, waits for them, and re-layouts  8.39 us

profile of v6, /device:TPU:1, one launch (start us, length us, event | category | flops | bytes accessed | tf_op | source)
XLA Modules:
  0.0 112.5 jit_solution(17935935434060277882)
XLA Ops:
  0.6 0.0 copy-start
  0.6 0.8 copy-done
  1.5 0.0 copy-start.1
  1.5 0.8 copy-done.1
  2.3 0.0 copy-start.2
  2.3 0.8 copy-done.2
  3.2 0.0 copy-start.3
  3.2 0.8 copy-done.3
  4.0 0.0 copy-start.4
  4.0 0.7 copy-done.4
  4.7 0.0 copy-start.6
  4.7 0.7 copy-done.6
  5.4 0.0 copy-start.5
  5.4 0.0 copy-start.7
  5.4 47.7 %gather.1 = (bf16[256,128]{1,0:T(8,128)(2,1)S(1)}, bf16[256,128]{1,0:T(8,128)(2,1)S(1)}, f32[264,128]{1,0:T(8,128)S(1)}, f32[264,128]{1,0:T(8,128)S(1)}, bf16[2,16,128,256]{3,2,1,0:T(8,128)(2,1)S(1)}) custom-call(bf16[32,1024]{1,0:T(8,128)(2,1)S(1)} %copy-done, bf16[32,1024]{1,0:T(8,128)(2,1)S(1)} %copy-done.1, bf16[32,1024]{1,0:T(8,128)(2,1)S(1)} %copy-done.2, ...), custom_call_target="tpu_custom_call" | custom-call | tf_op jit(solution)/shard_map/gather/pallas_call | solution.py:258
  53.1 10.9 %attention.1 = (bf16[256,128]{1,0:T(8,128)(2,1)S(1)}, bf16[256,128]{1,0:T(8,128)(2,1)S(1)}, bf16[4096,256]{1,0:T(8,128)(2,1)S(1)}) custom-call(bf16[256,128]{1,0:T(8,128)(2,1)S(1)} %get-tuple-element.14.q_ref, bf16[256,128]{1,0:T(8,128)(2,1)S(1)} %get-tuple-element.15.cot_ref, bf16[4096,256]{1,0:T(8,128)(2,1)S(1)} %bitcast.3), custom_call_target="tpu_custom_call" | custom-call | tf_op jit(solution)/shard_map/attention/pallas_call | solution.py:664
  64.0 0.0 copy-done.5
  64.0 0.0 copy-done.7
  64.0 44.8 %scatter.1 = (bf16[32,1024]{1,0:T(8,128)(2,1)S(1)}, bf16[32,1024]{1,0:T(8,128)(2,1)S(1)}, bf16[32,1024]{1,0:T(8,128)(2,1)S(1)}, bf16[32,1024]{1,0:T(8,128)(2,1)S...) custom-call(bf16[2,16,128,256]{3,2,1,0:T(8,128)(2,1)S(1)} %bitcast.2, bf16[256,128]{1,0:T(8,128)(2,1)S(1)} %get-tuple-element.18.att_in, ...), custom_call_target="tpu_custom_call" | custom-call | tf_op jit(solution)/shard_map/scatter/pallas_call | solution.py:553
  108.8 0.6 copy.18
  109.4 0.6 copy.19
  110.1 0.6 copy.20
  110.7 0.6 copy.21
  111.3 0.6 copy.22
  111.9 0.6 copy.23
Async XLA Ops:
  0.6 0.8 copy-start
  1.5 0.8 copy-start.1
  2.3 0.8 copy-start.2
  3.2 0.8 copy-start.3
  4.0 0.7 copy-start.4
  4.7 0.7 copy-start.6
  5.4 58.7 %copy-start.5 = (f32[3,128]{1,0:T(4,128)S(1)}, f32[3,128]{1,0:T(4,128)}, u32[]{:S(2)}) copy-start(f32[3,128]{1,0:T(4,128)} %kt.3) | copy-start | bytes 4612
  5.4 58.7 %copy-start.7 = (f32[3,128]{1,0:T(4,128)S(1)}, f32[3,128]{1,0:T(4,128)}, u32[]{:S(2)}) copy-start(f32[3,128]{1,0:T(4,128)} %vt.3) | copy-start | bytes 4612
